TPU v7x, 256 devices: a whole 4x4x8 slice. The times are simulated.
256 devices in a mesh: dp: 16 (over z, core), expert: 16 (over y, x).
Axes of the slice: x: 4, y: 4, z: 8, core: 2. Of those that a mesh axis runs over, the one named last changes fastest.
Arguments:
- tokens: bfloat16 [32768, 2048], P(('dp', 'expert')), may hold values from -6 to 6
- out_grad: bfloat16 [32768, 2048], P(('dp', 'expert')), may hold values from -1.5 to 1.5
- routes: int32 [32768, 2], P(('dp', 'expert')), may hold values from 0 to 15, all different within a row; in each aligned block of 128 rows (0 to 127, 128 to 255, ...) at most 32 rows name the same one
- route_probs: bfloat16 [32768, 2], P(('dp', 'expert')), may hold values from 0.049804688 to 1
- kept_count: int32 [16], P('dp'), may hold values from 512 to 2048, as said below
- gate_weight: bfloat16 [16, 2048, 768], P('expert', 'dp'), may hold values from -0.125 to 0.125
- up_weight: bfloat16 [16, 2048, 768], P('expert', 'dp'), may hold values from -0.125 to 0.125
- down_weight: bfloat16 [16, 2048, 768], P('expert', 'dp'), may hold values from -0.21875 to 0.21875
Outputs:
- token_grad: bfloat16 [32768, 2048], P(('dp', 'expert'))
- prob_grad: bfloat16 [32768, 2], P(('dp', 'expert'))
- weight_grad: bfloat16 [16, 2048, 2304], P('expert', 'dp')
Inputs may be any that keep to these rules, and one draw needn't show every extreme that they name: `routes`: among the rows of one device, no expert is named more than 32 times, and a row names 2 different experts. `kept_count`: rows of a data group whose index within the group is below its count are kept; in every draw some group keeps all its rows and another keeps a quarter of them.
All inputs are finite; a program needn't handle non-finite values.
Results may differ from a plain program's by a relative error of at most 0.018.
Values may be sent and summed in bfloat16 or wider, within the bound.
No kernel may reach another device: no remote copies, remote signals or barrier semaphores. Data moves between devices by JAX's collectives and lax.ppermute only.
A program may use at most 128 MiB of HBM per device.

v0:
```python
import jax
import jax.numpy as jnp
from jax import lax
from jax.sharding import PartitionSpec as P


def contract_rows(left, right):
    return lax.dot_general(
        left, right, (((0,), (0,)), ((), ())), preferred_element_type=jnp.float32
    )


def contract_last(left, right):
    return lax.dot_general(
        left, right, (((1,), (1,)), ((), ())), preferred_element_type=jnp.float32
    )


def per_device(
    tokens, out_grad, routes, route_probs, kept_count, gate_weight, up_weight, down_weight
):
    tok_rows, width = tokens.shape
    top = routes.shape[1]
    experts = lax.axis_size("expert")
    capacity = 2 * tok_rows * top // experts
    slots = experts * capacity
    gate_local = gate_weight[0]
    up_local = up_weight[0]
    down_local = down_weight[0]
    row = lax.axis_index("expert") * tok_rows + jnp.arange(tok_rows, dtype=jnp.int32)
    kept = row < kept_count[0]
    masked = jnp.where(kept[:, None], out_grad, jnp.zeros_like(out_grad))
    flat = routes.reshape(-1)
    onehot = (flat[:, None] == jnp.arange(experts, dtype=jnp.int32)[None, :]).astype(jnp.int32)
    before = jnp.cumsum(onehot, axis=0) - onehot
    position = jnp.sum(before * onehot, axis=1)
    target = (flat * capacity + position).reshape(tok_rows, top)
    match = target[None, :, :] == jnp.arange(slots, dtype=jnp.int32)[:, None, None]
    placing = jnp.any(match, axis=2).astype(jnp.bfloat16)
    send_rows = jnp.dot(placing, tokens, preferred_element_type=jnp.float32).astype(jnp.bfloat16)
    send_grad = jnp.dot(placing, masked, preferred_element_type=jnp.float32).astype(jnp.bfloat16)
    send_prob = jnp.sum(
        jnp.where(match, route_probs[None, :, :].astype(jnp.float32), 0.0), axis=(1, 2)
    ).astype(jnp.bfloat16)
    rows_in, grad_in, prob_in = (
        lax.all_to_all(send_rows, "expert", split_axis=0, concat_axis=0, tiled=True),
        lax.all_to_all(send_grad, "expert", split_axis=0, concat_axis=0, tiled=True),
        lax.all_to_all(send_prob, "expert", split_axis=0, concat_axis=0, tiled=True),
    )
    pieces = (
        lax.all_gather(gate_local, "dp", axis=0, tiled=True),
        lax.all_gather(up_local, "dp", axis=0, tiled=True),
    )
    pre_gate = jnp.dot(rows_in, pieces[0], preferred_element_type=jnp.float32)
    pre_up = jnp.dot(rows_in, pieces[1], preferred_element_type=jnp.float32)
    sig = jax.nn.sigmoid(pre_gate)
    act = (pre_gate * sig * pre_up).astype(jnp.bfloat16)
    scaled = (prob_in.astype(jnp.float32)[:, None] * grad_in.astype(jnp.float32)).astype(
        jnp.bfloat16
    )
    piece = lax.all_gather(down_local, "dp", axis=0, tiled=True)
    scaled_part = scaled
    output_part = contract_last(act, piece)
    back_hidden = jnp.dot(scaled_part, piece, preferred_element_type=jnp.float32)
    prob_part = jnp.sum(grad_in.astype(jnp.float32) * output_part, axis=1)
    d_gate = (back_hidden * pre_up * sig * (1.0 + pre_gate * (1.0 - sig))).astype(jnp.bfloat16)
    d_up = (back_hidden * pre_gate * sig).astype(jnp.bfloat16)
    stacked = jnp.stack((gate_local, up_local))
    pieces = lax.all_gather(stacked, "dp", axis=1, tiled=True)
    route_back = (contract_last(d_gate, pieces[0]) + contract_last(d_up, pieces[1])).astype(
        jnp.bfloat16
    )
    scaled_part = scaled
    summed = lax.psum_scatter(
        jnp.concatenate(
            (
                contract_rows(rows_in, d_gate),
                contract_rows(rows_in, d_up),
                contract_rows(scaled_part, act),
            ),
            axis=1,
        ).astype(jnp.bfloat16),
        "dp",
        scatter_dimension=0,
        tiled=True,
    )
    weight_grad = summed[None]
    rows_back, prob_back = (
        lax.all_to_all(route_back, "expert", split_axis=0, concat_axis=0, tiled=True),
        lax.all_to_all(
            prob_part.astype(jnp.bfloat16), "expert", split_axis=0, concat_axis=0, tiled=True
        ),
    )
    token_grad = contract_rows(placing, rows_back).astype(jnp.bfloat16)
    prob_grad = jnp.sum(
        jnp.where(match, prob_back.astype(jnp.float32)[:, None, None], 0.0), axis=0
    ).astype(jnp.bfloat16)
    return (token_grad, prob_grad, weight_grad)


def solution(mesh):
    in_specs = (
        P(("dp", "expert"), None),
        P(("dp", "expert"), None),
        P(("dp", "expert"), None),
        P(("dp", "expert"), None),
        P("dp"),
        P("expert", "dp", None),
        P("expert", "dp", None),
        P("expert", "dp", None),
    )
    out_specs = (P(("dp", "expert"), None), P(("dp", "expert"), None), P("expert", "dp", None))
    return jax.shard_map(
        per_device, mesh=mesh, in_specs=in_specs, out_specs=out_specs, check_vma=False
    )
```

profile of v0, /device:TPU:1, one launch (start us, length us, event | category | flops | bytes accessed | tf_op | source)
XLA Modules:
  0.0 269.6 jit_solution(16039769534471107603)
XLA Ops:
  7.2 0.7 all-gather.14.cloned.1.call-update
  8.0 0.7 all-gather.12.cloned.1.call-update
  8.7 0.7 all-gather.10.cloned.1.call-update
  9.5 1.8 pad_maximum_fusion.1
  11.3 0.8 copy.39
  12.1 0.1 eq.38
  12.2 0.1 eq.42
  12.4 0.6 reduce-window.6
  13.0 0.2 slice_reduce_fusion
  13.2 0.1 fusion.17
  13.3 0.1 reduce_sum.39
  13.5 0.1 fusion.12
  13.6 2.0 convolution_convert_fusion.3
  15.6 7.7 %all-to-all-start.2 = ((bf16[16,32,2048]{2,1,0:T(8,128)(2,1)}), bf16[16,32,2048]{2,1,0:T(8,128)(2,1)S(1)}, u32[]{:S(2)}, u32[]{:S(2)}) async-start(bf16[16,32,2048]{2,1,0:T(8,128)(2,1)} %bitcast.5), calls=%async_computation.2 | async-start | bytes 4194304 | tf_op jit(solution)/shard_map/all_to_all | solution.py:46
  24.0 2.2 convolution_convert_fusion.4
  26.2 27.6 %all-to-all-done.2 = bf16[16,32,2048]{2,1,0:T(8,128)(2,1)S(1)} async-done(((bf16[16,32,2048]{2,1,0:T(8,128)(2,1)}), bf16[16,32,2048]{2,1,0:T(8,128)(2,1)S(1)}, u32[]{:S(2)}, u32[]{:S(2)}) %all-to-all-start.2) | async-done | bytes 2097184 | tf_op jit(solution)/shard_map/all_to_all | solution.py:46
  53.8 1.3 copy-done.2
  55.1 4.3 %all-to-all-start.1 = ((bf16[16,32,2048]{2,1,0:T(8,128)(2,1)}), bf16[16,32,2048]{2,1,0:T(8,128)(2,1)S(1)}, u32[]{:S(2)}, u32[]{:S(2)}) async-start(bf16[16,32,2048]{2,1,0:T(8,128)(2,1)} %bitcast.72), calls=%async_computation.1 | async-start | bytes 4194304 | tf_op jit(solution)/shard_map/all_to_all | solution.py:47
  59.5 5.5 %fusion.4 = f32[512,768]{1,0:T(8,128)} fusion(bf16[512,2048]{1,0:T(8,128)(2,1)} %bitcast.75, bf16[1,2048,768]{2,1,0:T(8,128)(2,1)} %all-gather.14.cloned.1.call-done), kind=kOutput, calls=%fused_computation.13 | convolution fusion | flops 1610612736 | bytes 6815744 | tf_op jit(solution)/shard_map/dot_general | solution.py:54
  65.0 31.8 %all-gather.12.cloned.1.call-done = bf16[1,2048,768]{2,1,0:T(8,128)(2,1)} async-done(((bf16[1,128,768]{2,1,0:T(8,128)(2,1)}), bf16[1,2048,768]{2,1,0:T(8,128)(2,1)}) %all-gather.12.cloned.1.call-update) | async-done | bytes 3145744 | tf_op jit(solution)/shard_map/all_gather | solution.py:52
  96.8 5.9 %multiply_convert_fusion = (bf16[512,768]{1,0:T(8,128)(2,1)S(1)}, f32[512,768]{1,0:T(8,128)}) fusion(f32[512,768]{1,0:T(8,128)} %fusion.4, bf16[512,2048]{1,0:T(8,128)(2,1)} %bitcast.76, bf16[1,2048,768]{2,1,0:T(8,128)(2,1)} %all-gather.12.cloned.1.call-done), kind=kOutput, calls=%fused_computation.23 | convolution fusion | flops 1612972032 | bytes 9175040 | tf_op jit(solution)/shard_map/dot_general | solution.py:55
  102.7 35.5 %all-gather.10.cloned.1.call-done = bf16[1,2048,768]{2,1,0:T(8,128)(2,1)} async-done(((bf16[1,128,768]{2,1,0:T(8,128)(2,1)}), bf16[1,2048,768]{2,1,0:T(8,128)(2,1)}) %all-gather.10.cloned.1.call-update) | async-done | bytes 3145744 | tf_op jit(solution)/shard_map/all_gather | solution.py:61
  138.2 3.8 %fusion.1 = bf16[512]{0:T(512)(128)(2,1)S(1)} fusion(bf16[512,2048]{1,0:T(8,128)(2,1)S(1)} %bitcast.71, bf16[512,768]{1,0:T(8,128)(2,1)S(1)} %get-tuple-element.22, bf16[1,2048,768]{2,1,0:T(8,128)(2,1)} %all-gather.10.cloned.1.call-done), kind=kOutput, calls=%fused_computation.4 | convolution fusion | flops 1613757952 | bytes 6030336 | tf_op jit(solution)/shard_map/dot_general | solution.py:14
  142.1 0.7 convert_element_type.119
  142.8 6.5 %all-to-all-start.4 = ((bf16[16,32,1]{1,2,0:T(2,128)(2,1)}), bf16[16,32,1]{1,2,0:T(2,128)(2,1)S(1)}, u32[]{:S(2)}, u32[]{:S(2)}) async-start(bf16[16,32,1]{1,2,0:T(2,128)(2,1)} %convert_element_type.119), calls=%async_computation.4 | async-start | bytes 16384 | tf_op jit(solution)/shard_map/all_to_all | solution.py:90
  149.4 6.3 %all-to-all-done.4 = bf16[16,32,1]{1,2,0:T(2,128)(2,1)S(1)} async-done(((bf16[16,32,1]{1,2,0:T(2,128)(2,1)}), bf16[16,32,1]{1,2,0:T(2,128)(2,1)S(1)}, u32[]{:S(2)}, u32[]{:S(2)}) %all-to-all-start.4) | async-done | bytes 1056 | tf_op jit(solution)/shard_map/all_to_all | solution.py:90
  155.7 0.1 reshape.88
  155.7 0.7 select_reduce_fusion
  156.4 0.1 convert_element_type.118
  156.5 9.1 %all_to_all.45 = bf16[16,32,1]{1,2,0:T(2,128)(2,1)S(1)} all-to-all(bf16[16,32,1]{1,2,0:T(2,128)(2,1)S(1)} %convert_element_type.118), channel_id=1, replica_groups=mesh['dp'=16,'expert'=16] {'expert'}, dimensions={0} | all-to-all | bytes 2048 | tf_op jit(solution)/shard_map/all_to_all | solution.py:48
  165.7 0.1 reshape.86
  165.7 0.4 fusion
  166.2 1.9 convolution_convert_fusion
  168.1 0.1 copy-done.7
  168.1 0.5 copy-done.9
  168.6 0.5 copy-done.10
  169.1 2.1 multiply_convert_fusion.2
  171.2 1.9 convolution_convert_fusion.1
  173.1 1.9 convolution_convert_fusion.2
  175.0 4.5 %pad_maximum_fusion = bf16[2048,2304]{0,1:T(8,128)(2,1)} fusion(bf16[2048,768]{0,1:T(8,128)(2,1)S(1)} %convolution_convert_fusion, bf16[2048,768]{0,1:T(8,128)(2,1)S(1)} %convolution_convert_fusion.1, bf16[2048,768]{0,1:T(8,128)(2,1)S(1)} %convolution_convert_fusion.2), kind=kLoop, calls=%fused_computation | loop fusion | flops 28311552 | bytes 18874368 | tf_op jit(solution)/shard_map/concatenate | solution.py:75
  179.5 12.5 %copy.46 = bf16[2048,2304]{1,0:T(8,128)(2,1)} copy(bf16[2048,2304]{0,1:T(8,128)(2,1)} %pad_maximum_fusion) | data formatting | bytes 18874368
  192.1 3.9 %fusion.2 = f32[512,2048]{1,0:T(8,128)S(1)} fusion(bf16[512,768]{1,0:T(8,128)(2,1)S(1)} %get-tuple-element.21, bf16[2,2048,768]{2,1,0:T(8,128)(2,1)} %all-gather.8.cloned.1.call-done), kind=kOutput, calls=%fused_computation.10 | convolution fusion | flops 1610612736 | bytes 8126464 | tf_op jit(solution)/shard_map/dot_general | solution.py:14
  196.0 1.9 add_convert_fusion
  197.8 28.5 %all_to_all.46 = bf16[16,32,2048]{2,1,0:T(8,128)(2,1)S(1)} all-to-all(bf16[16,32,2048]{2,1,0:T(8,128)(2,1)S(1)} %bitcast.79), channel_id=1, replica_groups=mesh['dp'=16,'expert'=16] {'expert'}, dimensions={0} | all-to-all | bytes 4194304 | tf_op jit(solution)/shard_map/all_to_all | solution.py:89
  226.3 1.3 convolution_convert_fusion.5
  227.6 33.1 %reduce-scatter.4.cloned.1.call-done = bf16[128,2304]{1,0:T(8,128)(2,1)} async-done(((bf16[2048,2304]{1,0:T(8,128)(2,1)}), bf16[128,2304]{1,0:T(8,128)(2,1)}) %reduce-scatter.4.cloned.1.call-update) | async-done | bytes 589840
  260.7 1.4 copy.47
  262.0 1.1 copy.45
  (37 shorter events, 0.5 us)
Async XLA Ops:
  7.2 6.4 %copy-start = (bf16[128,2048]{1,0:T(8,128)(2,1)S(1)}, bf16[128,2048]{1,0:T(8,128)(2,1)}, u32[]{:S(2)}) copy-start(bf16[128,2048]{1,0:T(8,128)(2,1)} %param.8) | copy-start | bytes 1572868
  7.2 6.3 %copy-start.5 = (s32[128,2]{0,1:T(2,128)S(1)}, s32[128,2]{0,1:T(2,128)}, u32[]{:S(2)}) copy-start(s32[128,2]{0,1:T(2,128)} %param.10) | copy-start | bytes 3076
  7.2 52.3 %all-gather.14.cloned.1.call-start = ((), (), s32[]{:S(2)}) async-start(), calls=%async_computation.9 | async-start | bytes 3342336 | tf_op jit(solution)/shard_map/all_gather | solution.py:51
  7.9 88.8 %all-gather.12.cloned.1.call-start = ((), (), s32[]{:S(2)}) async-start(), calls=%async_computation.8 | async-start | bytes 3342336 | tf_op jit(solution)/shard_map/all_gather | solution.py:52
  8.7 129.5 %all-gather.10.cloned.1.call-start = ((), (), s32[]{:S(2)}) async-start(), calls=%async_computation.7 | async-start | bytes 3342336 | tf_op jit(solution)/shard_map/all_gather | solution.py:61
  9.4 182.6 %all-gather.8.cloned.1.call-start = ((), (), s32[]{:S(2)}) async-start(), calls=%async_computation.6 | async-start | bytes 6684672 | tf_op jit(solution)/shard_map/all_gather | solution.py:69
  15.6 8.4 %copy-start.4 = (bf16[128,2048]{1,0:T(8,128)(2,1)S(1)}, bf16[128,2048]{1,0:T(8,128)(2,1)}, u32[]{:S(2)}) copy-start(bf16[128,2048]{1,0:T(8,128)(2,1)} %param.9) | copy-start | bytes 1572868
  15.6 38.2 %all-to-all-start.2 = ((bf16[16,32,2048]{2,1,0:T(8,128)(2,1)}), bf16[16,32,2048]{2,1,0:T(8,128)(2,1)S(1)}, u32[]{:S(2)}, u32[]{:S(2)}) async-start(bf16[16,32,2048]{2,1,0:T(8,128)(2,1)} %bitcast.5), calls=%async_computation.2 | async-start | bytes 4194304 | tf_op jit(solution)/shard_map/all_to_all | solution.py:46
  53.8 1.3 copy-start.2
  55.1 47.5 %all-to-all-start.1 = ((bf16[16,32,2048]{2,1,0:T(8,128)(2,1)}), bf16[16,32,2048]{2,1,0:T(8,128)(2,1)S(1)}, u32[]{:S(2)}, u32[]{:S(2)}) async-start(bf16[16,32,2048]{2,1,0:T(8,128)(2,1)} %bitcast.72), calls=%async_computation.1 | async-start | bytes 4194304 | tf_op jit(solution)/shard_map/all_to_all | solution.py:47
  138.2 11.1 %copy-start.8 = (bf16[128,2]{0,1:T(2,128)(2,1)S(1)}, bf16[128,2]{0,1:T(2,128)(2,1)}, u32[]{:S(2)}) copy-start(bf16[128,2]{0,1:T(2,128)(2,1)} %param.11) | copy-start | bytes 1540
  142.8 12.9 %all-to-all-start.4 = ((bf16[16,32,1]{1,2,0:T(2,128)(2,1)}), bf16[16,32,1]{1,2,0:T(2,128)(2,1)S(1)}, u32[]{:S(2)}, u32[]{:S(2)}) async-start(bf16[16,32,1]{1,2,0:T(2,128)(2,1)} %convert_element_type.119), calls=%async_computation.4 | async-start | bytes 16384 | tf_op jit(solution)/shard_map/all_to_all | solution.py:90
  149.3 111.4 %reduce-scatter.4.cloned.1.call-start = ((), (), s32[]{:S(2)}) async-start(), calls=%async_computation.10 | async-start | bytes 10027008
  166.2 2.0 copy-start.7
  166.2 2.4 copy-start.9
  166.2 2.9 %copy-start.10 = (f32[512,768]{1,0:T(8,128)S(1)}, f32[512,768]{1,0:T(8,128)}, u32[]{:S(2)}) copy-start(f32[512,768]{1,0:T(8,128)} %get-tuple-element.23) | copy-start | bytes 4718596
  169.1 2.1 copy-start.3
  192.1 3.9 %copy-start.6 = (bf16[2,2048,768]{2,1,0:T(8,128)(2,1)S(1)}, bf16[2,2048,768]{2,1,0:T(8,128)(2,1)}, u32[]{:S(2)}) copy-start(bf16[2,2048,768]{2,1,0:T(8,128)(2,1)} %all-gather.8.cloned.1.call-done) | copy-start | bytes 18874372
  226.3 36.8 %copy-start.1 = (bf16[128,2048]{1,0:T(8,128)(2,1)S(1)}, bf16[128,2048]{1,0:T(8,128)(2,1)}, u32[]{:S(2)}) copy-start(bf16[128,2048]{1,0:T(8,128)(2,1)} %param.8) | copy-start | bytes 1572868
Sparse Core Ops, SparseCore 0:
  9.9 45.1 all-gather.13
  56.9 39.8 all-gather.11
  98.6 39.5 all-gather.9
  140.5 44.6 all-gather.7
  192.2 68.4 reduce-scatter.3
where the time goes:
time: 272 us; the launch traced here: 270 us
  waiting for transfers between devices  136 us (50%)
  blocking collectives  37.6 us (14%)
  matrix products  34.1 us (13%)
  local copies, waits for them, and re-layouts  19.8 us (7%)
  starting transfers between devices  18.8 us (7%)
  between operations  14.7 us (5%)
  other arithmetic  8.25 us (3%)
    all_gather x1, waiting for transfers between devices, per_device(): piece = lax.all_gather(down_local, 'dp', axis=0, tiled=True)  35.5 us
    unnamed x6, waiting for transfers between devices  35.2 us
    all_gather x1, waiting for transfers between devices, per_device(): lax.all_gather(up_local, 'dp', axis=0, tiled=True)  31.8 us
    all_to_all x1, blocking collectives, per_device(): lax.all_to_all(route_back, 'expert', split_axis=0, concat_axis=0, tiled=T...  28.5 us
    all_to_all x1, waiting for transfers between devices, per_device(): lax.all_to_all(send_rows, 'expert', split_axis=0, concat_axis=0, tiled=True)  27.6 us
    unnamed x26, local copies, waits for them, and re-layouts  18.2 us
    dot_general x3, matrix products, contract_last(): lax.dot_general(left, right, (((1,), (1,)), ((), ())), preferred_element_...  9.55 us
    all_to_all x1, blocking collectives, per_device(): lax.all_to_all(send_prob, 'expert', split_axis=0, concat_axis=0, tiled=True)  9.12 us
  transfers between devices with their start and end apart: 8, of which 5 were waited for; matrix products, arithmetic and copies ran while one was open for 21% of the time, Pallas kernels for 0%

commit v1 on v0

v1 whole, which is shorter than its diff:
```python
import jax
import jax.numpy as jnp
from jax import lax
from jax.sharding import PartitionSpec as P


def contract_rows(left, right):
    return lax.dot_general(
        left, right, (((0,), (0,)), ((), ())), preferred_element_type=jnp.float32
    )


def contract_last(left, right):
    return lax.dot_general(
        left, right, (((1,), (1,)), ((), ())), preferred_element_type=jnp.float32
    )


def per_device(
    tokens, out_grad, routes, route_probs, kept_count, gate_weight, up_weight, down_weight
):
    tok_rows, width = tokens.shape
    top = routes.shape[1]
    experts = lax.axis_size("expert")
    capacity = 2 * tok_rows * top // experts
    slots = experts * capacity
    weights = lax.all_gather(
        jnp.concatenate((gate_weight, up_weight, down_weight), axis=0), "dp", axis=1, tiled=True
    )
    row = lax.axis_index("expert") * tok_rows + jnp.arange(tok_rows, dtype=jnp.int32)
    kept = row < kept_count[0]
    masked = jnp.where(kept[:, None], out_grad, jnp.zeros_like(out_grad))
    flat = routes.reshape(-1)
    onehot = (flat[:, None] == jnp.arange(experts, dtype=jnp.int32)[None, :]).astype(jnp.int32)
    before = jnp.cumsum(onehot, axis=0) - onehot
    position = jnp.sum(before * onehot, axis=1)
    target = (flat * capacity + position).reshape(tok_rows, top)
    slot = jnp.arange(slots, dtype=jnp.int32)[:, None]
    probs = route_probs.astype(jnp.float32)
    match = [slot == target[None, :, k] for k in range(top)]
    placing = (match[0] | match[1]).astype(jnp.bfloat16)
    weighted = (
        jnp.where(match[0], probs[None, :, 0], 0.0) + jnp.where(match[1], probs[None, :, 1], 0.0)
    ).astype(jnp.bfloat16)
    send_rows = jnp.dot(placing, tokens, preferred_element_type=jnp.float32).astype(jnp.bfloat16)
    send_scaled = jnp.dot(weighted, masked, preferred_element_type=jnp.float32).astype(jnp.bfloat16)
    rows_in = lax.all_to_all(send_rows, "expert", split_axis=0, concat_axis=0, tiled=True)
    scaled = lax.all_to_all(send_scaled, "expert", split_axis=0, concat_axis=0, tiled=True)
    pre_gate = jnp.dot(rows_in, weights[0], preferred_element_type=jnp.float32)
    pre_up = jnp.dot(rows_in, weights[1], preferred_element_type=jnp.float32)
    sig = jax.nn.sigmoid(pre_gate)
    act = (pre_gate * sig * pre_up).astype(jnp.bfloat16)
    back_hidden = jnp.dot(scaled, weights[2], preferred_element_type=jnp.float32)
    prob_part = jnp.sum(act.astype(jnp.float32) * back_hidden, axis=1)
    d_gate = (back_hidden * pre_up * sig * (1.0 + pre_gate * (1.0 - sig))).astype(jnp.bfloat16)
    d_up = (back_hidden * pre_gate * sig).astype(jnp.bfloat16)
    weight_grad = lax.psum_scatter(
        jnp.concatenate(
            (
                contract_rows(rows_in, d_gate),
                contract_rows(rows_in, d_up),
                contract_rows(scaled, act),
            ),
            axis=1,
        ).astype(jnp.bfloat16),
        "dp",
        scatter_dimension=0,
        tiled=True,
    )[None]
    route_back = (contract_last(d_gate, weights[0]) + contract_last(d_up, weights[1])).astype(
        jnp.bfloat16
    )
    prob_all = lax.all_gather(
        prob_part.astype(jnp.bfloat16).reshape(experts, capacity), "expert", axis=0, tiled=False
    )
    rows_back = lax.all_to_all(route_back, "expert", split_axis=0, concat_axis=0, tiled=True)
    prob_back = lax.dynamic_index_in_dim(
        prob_all, lax.axis_index("expert"), axis=1, keepdims=False
    ).reshape(slots)
    token_grad = contract_rows(placing, rows_back).astype(jnp.bfloat16)
    prob_grad = jnp.stack(
        [jnp.sum(jnp.where(m, prob_back.astype(jnp.float32)[:, None], 0.0), axis=0) for m in match],
        axis=1,
    )
    prob_grad = (prob_grad / probs).astype(jnp.bfloat16)
    return (token_grad, prob_grad, weight_grad)


def solution(mesh):
    in_specs = (
        P(("dp", "expert"), None),
        P(("dp", "expert"), None),
        P(("dp", "expert"), None),
        P(("dp", "expert"), None),
        P("dp"),
        P("expert", "dp", None),
        P("expert", "dp", None),
        P("expert", "dp", None),
    )
    out_specs = (P(("dp", "expert"), None), P(("dp", "expert"), None), P("expert", "dp", None))
    return jax.shard_map(
        per_device, mesh=mesh, in_specs=in_specs, out_specs=out_specs, check_vma=False
    )
```

time: 272 us -> 199 us (0.73)
  waiting for transfers between devices: 136 us -> 57.3 us
  blocking collectives: 37.6 us -> 42.5 us
  matrix products: 34.1 us -> 37.2 us
    all_gather x4 -> x1, waiting for transfers between devices: 67.4 us -> 19.1 us  [per_device(): lax.all_gather(jnp.concatenate((gate_weight, up_weight, down_weight), axi...]
    all_gather x0 -> x1, blocking collectives: none -> 42.5 us  [per_device(): lax.all_gather(prob_part.astype(jnp.bfloat16).reshape(experts, capacity),...]
    all_to_all x2 -> x0, blocking collectives: 37.6 us -> none  [the longest x1 28.5 us: per_device(): lax.all_to_all(route_back, 'expert', split_axis=0, concat_axis=0, tiled=T...]
    unnamed x6 -> x3, waiting for transfers between devices: 35.2 us -> 10.6 us
    all_to_all x2, waiting for transfers between devices: 6.26 us -> 0.01 us  [the longest x1 0.01 us: per_device(): lax.all_to_all(send_scaled, 'expert', split_axis=0, concat_axis=0, tiled=...]
    unnamed x26 -> x16, local copies, waits for them, and re-layouts: 18.2 us -> 16.6 us
    dot_general x3 -> x2, matrix products: 9.55 us -> 8.76 us  [contract_last(): lax.dot_general(left, right, (((1,), (1,)), ((), ())), preferred_element_...]
  transfers between devices with their start and end apart: 8 -> 5, of which waited for: 5 -> 3; matrix products, arithmetic and copies ran while one was open for 21% -> 14% of each run, Pallas kernels for 0% -> 0%
where the time goes in v1:
time: 199 us; the launch traced here: 196 us
  waiting for transfers between devices  57.3 us (29%)
  blocking collectives  42.5 us (21%)
  matrix products  37.2 us (19%)
  starting transfers between devices  19 us (10%)
  local copies, waits for them, and re-layouts  17.4 us (9%)
  between operations  14.9 us (7%)
  other arithmetic  8.16 us (4%)
    all_gather x1, blocking collectives, per_device(): lax.all_gather(prob_part.astype(jnp.bfloat16).reshape(experts, capacity),...  42.5 us
    all_to_all x1, waiting for transfers between devices, per_device(): lax.all_to_all(send_rows, 'expert', split_axis=0, concat_axis=0, tiled=True)  27.6 us
    all_gather x1, waiting for transfers between devices, per_device(): lax.all_gather(jnp.concatenate((gate_weight, up_weight, down_weight), axi...  19.1 us
    unnamed x16, local copies, waits for them, and re-layouts  16.6 us
    unnamed x3, waiting for transfers between devices  10.6 us
    dot_general x2, matrix products, contract_last(): lax.dot_general(left, right, (((1,), (1,)), ((), ())), preferred_element_...  8.76 us
    dot_general x4, matrix products, contract_rows(): lax.dot_general(left, right, (((0,), (0,)), ((), ())), preferred_element_...  8.75 us
    all_to_all x1, starting transfers between devices, per_device(): lax.all_to_all(send_rows, 'expert', split_axis=0, concat_axis=0, tiled=True)  7.72 us
  transfers between devices with their start and end apart: 5, of which 3 were waited for; matrix products, arithmetic and copies ran while one was open for 14% of the time, Pallas kernels for 0%

profile of v1, /device:TPU:1, one launch (start us, length us, event | category | flops | bytes accessed | tf_op | source)
XLA Modules:
  0.0 196.5 jit_solution(17751260392276215805)
XLA Ops:
  7.2 0.0 copy-start
  7.2 0.0 copy-start.2
  7.2 0.0 all-gather.2.cloned.1.call-start
  7.2 2.0 %pad_maximum_fusion.1 = bf16[3,128,768]{2,1,0:T(8,128)(2,1)} fusion(bf16[1,128,768]{2,1,0:T(8,128)(2,1)} %param.15, bf16[1,128,768]{2,1,0:T(8,128)(2,1)} %param.14, bf16[1,128,768]{2,1,0:T(8,128)(2,1)} %param.13), kind=kLoop, calls=%fused_computation.20 | loop fusion | flops 589824 | bytes 1179648 | tf_op jit(solution)/shard_map/concatenate | solution.py:28
  9.3 0.0 all-gather.2.cloned.1.call-update
  9.3 0.8 copy.36
  10.1 0.1 eq.56
  10.2 0.1 eq.60
  10.4 0.6 reduce-window.6
  11.0 0.2 slice_reduce_fusion
  11.2 0.1 fusion.21
  11.3 0.1 reduce_sum.39
  11.4 0.1 copy.39
  11.5 0.0 copy-done.2
  11.5 0.0 copy-done
  11.6 2.0 %convolution_convert_fusion.4 = bf16[512,2048]{1,0:T(8,128)(2,1)} fusion(bf16[128,2048]{1,0:T(8,128)(2,1)S(1)} %copy-done, s32[128]{0:T(128)S(1)} %get-tuple-element.30, s32[128]{0:T(128)S(1)} %get-tuple-element.29), kind=kOutput, calls=%fused_computation.10 | convolution fusion | flops 269680640 | bytes 2622464 | tf_op jit(solution)/shard_map/dot_general | solution.py:45
  13.6 7.7 %all-to-all-start.1 = ((bf16[16,32,2048]{2,1,0:T(8,128)(2,1)}), bf16[16,32,2048]{2,1,0:T(8,128)(2,1)S(1)}, u32[]{:S(2)}, u32[]{:S(2)}) async-start(bf16[16,32,2048]{2,1,0:T(8,128)(2,1)} %bitcast.9), calls=%async_computation.1 | async-start | bytes 4194304 | tf_op jit(solution)/shard_map/all_to_all | solution.py:47
  22.0 0.0 copy-done.1
  22.0 2.2 %convolution_convert_fusion.3 = bf16[512,2048]{1,0:T(8,128)(2,1)} fusion(bf16[128,2048]{1,0:T(8,128)(2,1)S(1)} %copy-done.1, pred[128]{0:T(512)(128)(4,1)S(1)} %add_compare_fusion, f32[128]{0:T(128)S(1)} %get-tuple-element.28, f32[128]{0:T(128)S(1)} %get-tuple-element.27, s32[128]{0:T(128)S(1)} %get-tuple-element.30, s32[128]{0:T(128)S(1)} %get-tuple-element.29), kind=kOutput, calls=%fused_computation.9 | convolution fusion | flops 270139392 | bytes 2623616 | tf_op jit(solution)/shard_map/dot_general | solution.py:46
  24.2 27.6 %all-to-all-done.1 = bf16[16,32,2048]{2,1,0:T(8,128)(2,1)S(1)} async-done(((bf16[16,32,2048]{2,1,0:T(8,128)(2,1)}), bf16[16,32,2048]{2,1,0:T(8,128)(2,1)S(1)}, u32[]{:S(2)}, u32[]{:S(2)}) %all-to-all-start.1) | async-done | bytes 2097184 | tf_op jit(solution)/shard_map/all_to_all | solution.py:47
  51.8 4.4 %all-to-all-start = ((bf16[16,32,2048]{2,1,0:T(8,128)(2,1)}), bf16[16,32,2048]{2,1,0:T(8,128)(2,1)}, u32[]{:S(2)}, u32[]{:S(2)}) async-start(bf16[16,32,2048]{2,1,0:T(8,128)(2,1)} %bitcast.6), calls=%async_computation | async-start | bytes 4194304 | tf_op jit(solution)/shard_map/all_to_all | solution.py:48
  56.3 0.2 reduce-scatter.4.cloned.1.call-start
  56.5 19.1 %all-gather.2.cloned.1.call-done = bf16[3,2048,768]{2,1,0:T(8,128)(2,1)} async-done(((bf16[3,128,768]{2,1,0:T(8,128)(2,1)}), bf16[3,2048,768]{2,1,0:T(8,128)(2,1)}) %all-gather.2.cloned.1.call-update) | async-done | bytes 9437200 | tf_op jit(solution)/shard_map/all_gather | solution.py:27
  75.6 4.8 %fusion.1 = f32[512,768]{1,0:T(8,128)} fusion(bf16[512,2048]{1,0:T(8,128)(2,1)S(1)} %bitcast.67, bf16[3,2048,768]{2,1,0:T(8,128)(2,1)} %all-gather.2.cloned.1.call-done), kind=kOutput, calls=%fused_computation.11 | convolution fusion | flops 1610612736 | bytes 6815744 | tf_op jit(solution)/shard_map/dot_general | solution.py:50
  80.4 4.9 %fusion.3 = f32[512,768]{1,0:T(8,128)} fusion(bf16[512,2048]{1,0:T(8,128)(2,1)S(1)} %bitcast.68, bf16[3,2048,768]{2,1,0:T(8,128)(2,1)} %all-gather.2.cloned.1.call-done), kind=kOutput, calls=%fused_computation.13 | convolution fusion | flops 1610612736 | bytes 6815744 | tf_op jit(solution)/shard_map/dot_general | solution.py:49
  85.3 0.0 all-to-all-done
  85.3 5.8 %multiply_reduce_fusion = (bf16[512]{0:T(512)(128)(2,1)S(1)}, bf16[512,768]{1,0:T(8,128)(2,1)S(1)}, bf16[512,768]{1,0:T(8,128)(2,1)S(1)}, bf16[512,768]{1,0:T(8,128)(2,1)S(1)}) fusion(f32[512,768]{1,0:T(8,128)} %fusion.1, f32[512,768]{1,0:T(8,128)} %fusion.3, bf16[512,2048]{1,0:T(8,128)(2,1)} %bitcast.7, bf16[3,2048,768]{2,1,0:T(8,128)(2,1)} %all-gather.2.cloned.1.call-done), kind=kOutput, calls=%fused_computation.15 | convolution fusion | flops 1618083328 | bytes 10748928 | tf_op jit(solution)/shard_map/dot_general | solution.py:53
  91.1 3.7 %convolution_convert_fusion = bf16[2048,768]{0,1:T(8,128)(2,1)S(1)} fusion(bf16[512,2048]{1,0:T(8,128)(2,1)} %bitcast.7, bf16[512,768]{1,0:T(8,128)(2,1)S(1)} %get-tuple-element.24), kind=kOutput, calls=%fused_computation.2 | convolution fusion | flops 1612185600 | bytes 6029312 | tf_op jit(solution)/shard_map/dot_general | solution.py:8
  94.8 1.9 convolution_convert_fusion.1
  96.7 0.0 copy-done.4
  96.7 1.9 convolution_convert_fusion.2
  98.6 4.7 %pad_maximum_fusion = bf16[2048,2304]{0,1:T(8,128)(2,1)} fusion(bf16[2048,768]{0,1:T(8,128)(2,1)S(1)} %convolution_convert_fusion, bf16[2048,768]{0,1:T(8,128)(2,1)S(1)} %convolution_convert_fusion.1, bf16[2048,768]{0,1:T(8,128)(2,1)S(1)} %convolution_convert_fusion.2), kind=kLoop, calls=%fused_computation | loop fusion | flops 28311552 | bytes 18874368 | tf_op jit(solution)/shard_map/concatenate | solution.py:58
  103.2 12.2 %copy.41 = bf16[2048,2304]{1,0:T(8,128)(2,1)} copy(bf16[2048,2304]{0,1:T(8,128)(2,1)} %pad_maximum_fusion) | data formatting | bytes 18874368
  115.5 0.0 reduce-scatter.4.cloned.1.call-update
  115.5 1.1 copy-done.5
  116.6 3.7 %fusion.2 = f32[512,2048]{1,0:T(8,128)S(1)} fusion(bf16[512,768]{1,0:T(8,128)(2,1)S(1)} %copy-done.5, bf16[3,2048,768]{2,1,0:T(8,128)(2,1)} %all-gather.2.cloned.1.call-done), kind=kOutput, calls=%fused_computation.12 | convolution fusion | flops 1610612736 | bytes 8126464 | tf_op jit(solution)/shard_map/dot_general | solution.py:14
  120.3 5.0 %add_convert_fusion = bf16[512,2048]{1,0:T(8,128)(2,1)} fusion(f32[512,2048]{1,0:T(8,128)S(1)} %fusion.2, bf16[512,768]{1,0:T(8,128)(2,1)S(1)} %get-tuple-element.26, bf16[3,2048,768]{2,1,0:T(8,128)(2,1)} %all-gather.2.cloned.1.call-done), kind=kOutput, calls=%fused_computation.1 | convolution fusion | flops 1612709888 | bytes 10223616 | tf_op jit(solution)/shard_map/dot_general | solution.py:14
  125.4 6.5 %all-to-all-start.2 = ((bf16[16,32,2048]{2,1,0:T(8,128)(2,1)}), bf16[16,32,2048]{2,1,0:T(8,128)(2,1)S(1)}, u32[]{:S(2)}, u32[]{:S(2)}) async-start(bf16[16,32,2048]{2,1,0:T(8,128)(2,1)} %bitcast.71), calls=%async_computation.2 | async-start | bytes 4194304 | tf_op jit(solution)/shard_map/all_to_all | solution.py:76
  131.9 0.1 convert_element_type.79
  132.0 42.5 %all_gather.7 = bf16[16,16,32]{2,1,0:T(8,128)(2,1)S(1)} all-gather(bf16[1,16,32]{2,1,0:T(8,128)(2,1)S(1)} %convert_element_type.79), channel_id=1, replica_groups=mesh['dp'=16,'expert'=16] {'expert'}, dimensions={0}, use_global_device_ids=true | all-gather | bytes 17408 | tf_op jit(solution)/shard_map/all_gather | solution.py:73
  174.5 0.1 reshape.62
  174.6 0.2 select_reduce_fusion.1
  174.8 0.5 fusion.23
  175.3 0.0 all-to-all-done.2
  175.3 1.3 convolution_convert_fusion.5
  176.6 10.6 %reduce-scatter.4.cloned.1.call-done = bf16[128,2304]{1,0:T(8,128)(2,1)} async-done(((bf16[2048,2304]{1,0:T(8,128)(2,1)}), bf16[128,2304]{1,0:T(8,128)(2,1)}) %reduce-scatter.4.cloned.1.call-update) | async-done | bytes 589840
  187.2 1.4 copy.42
  188.5 1.1 copy.40
  (14 shorter events, 0.1 us)
Async XLA Ops:
  7.2 4.4 %copy-start = (bf16[128,2048]{1,0:T(8,128)(2,1)S(1)}, bf16[128,2048]{1,0:T(8,128)(2,1)}, u32[]{:S(2)}) copy-start(bf16[128,2048]{1,0:T(8,128)(2,1)} %param.8) | copy-start | bytes 1572868
  7.2 4.3 %copy-start.2 = (s32[128,2]{0,1:T(2,128)S(1)}, s32[128,2]{0,1:T(2,128)}, u32[]{:S(2)}) copy-start(s32[128,2]{0,1:T(2,128)} %param.10) | copy-start | bytes 3076
  7.2 68.4 %all-gather.2.cloned.1.call-start = ((), (), s32[]{:S(2)}) async-start(), calls=%async_computation.4 | async-start | bytes 10027008 | tf_op jit(solution)/shard_map/all_gather | solution.py:27
  13.6 8.4 %copy-start.3 = (bf16[128,2]{0,1:T(2,128)(2,1)S(1)}, bf16[128,2]{0,1:T(2,128)(2,1)}, u32[]{:S(2)}) copy-start(bf16[128,2]{0,1:T(2,128)(2,1)} %param.11) | copy-start | bytes 1540
  13.6 8.4 %copy-start.1 = (bf16[128,2048]{1,0:T(8,128)(2,1)S(1)}, bf16[128,2048]{1,0:T(8,128)(2,1)}, u32[]{:S(2)}) copy-start(bf16[128,2048]{1,0:T(8,128)(2,1)} %param.9) | copy-start | bytes 1572868
  13.6 38.2 %all-to-all-start.1 = ((bf16[16,32,2048]{2,1,0:T(8,128)(2,1)}), bf16[16,32,2048]{2,1,0:T(8,128)(2,1)S(1)}, u32[]{:S(2)}, u32[]{:S(2)}) async-start(bf16[16,32,2048]{2,1,0:T(8,128)(2,1)} %bitcast.9), calls=%async_computation.1 | async-start | bytes 4194304 | tf_op jit(solution)/shard_map/all_to_all | solution.py:47
  51.8 33.5 %all-to-all-start = ((bf16[16,32,2048]{2,1,0:T(8,128)(2,1)}), bf16[16,32,2048]{2,1,0:T(8,128)(2,1)}, u32[]{:S(2)}, u32[]{:S(2)}) async-start(bf16[16,32,2048]{2,1,0:T(8,128)(2,1)} %bitcast.6), calls=%async_computation | async-start | bytes 4194304 | tf_op jit(solution)/shard_map/all_to_all | solution.py:48
  56.3 130.9 %reduce-scatter.4.cloned.1.call-start = ((), (), s32[]{:S(2)}) async-start(), calls=%async_computation.5 | async-start | bytes 10027008
  91.1 5.6 %copy-start.4 = (bf16[512,768]{1,0:T(8,128)(2,1)}, bf16[512,768]{1,0:T(8,128)(2,1)S(1)}, u32[]{:S(2)}) copy-start(bf16[512,768]{1,0:T(8,128)(2,1)S(1)} %get-tuple-element.25) | copy-start | bytes 2359300
  115.5 1.1 copy-start.5
  125.4 49.9 %all-to-all-start.2 = ((bf16[16,32,2048]{2,1,0:T(8,128)(2,1)}), bf16[16,32,2048]{2,1,0:T(8,128)(2,1)S(1)}, u32[]{:S(2)}, u32[]{:S(2)}) async-start(bf16[16,32,2048]{2,1,0:T(8,128)(2,1)} %bitcast.71), calls=%async_computation.2 | async-start | bytes 4194304 | tf_op jit(solution)/shard_map/all_to_all | solution.py:76
Sparse Core Ops, SparseCore 0:
  10.4 65.0 all-gather.1
  115.6 71.5 reduce-scatter.3

commit v2 on v1

v2 whole, which is shorter than its diff:
```python
import jax
import jax.numpy as jnp
from jax import lax
from jax.experimental import pallas as pl
from jax.experimental.pallas import tpu as pltpu
from jax.sharding import PartitionSpec as P

F32 = jnp.float32
BF16 = jnp.bfloat16
VMEM_LIMIT = 56 * 1024 * 1024
LANES = 128
BLOCK = 256


def dot(left, right):
    return jnp.dot(left, right, preferred_element_type=F32)


def dot_rows(left, right):
    return lax.dot_general(left, right, (((0,), (0,)), ((), ())), preferred_element_type=F32)


def dot_last(left, right):
    return lax.dot_general(left, right, (((1,), (1,)), ((), ())), preferred_element_type=F32)


def params():
    return pltpu.CompilerParams(
        vmem_limit_bytes=VMEM_LIMIT, dimension_semantics=("arbitrary",)
    )


def hidden(received, weights):
    experts, _, capacity, width = received.shape
    slots, ff = experts * capacity, weights.shape[2]

    def body(rows_ref, scaled_ref, w_ref, grads_ref, act_ref, prob_ref, rows_out, scaled_out):
        rows = rows_ref[...].reshape(slots, width)
        scaled = scaled_ref[...].reshape(slots, width)
        gate = dot(rows, w_ref[0])
        up = dot(rows, w_ref[1])
        back = dot(scaled, w_ref[2])
        sig = jax.nn.sigmoid(gate)
        silu = gate * sig
        act = (silu * up).astype(BF16)
        grads_ref[:, :BLOCK] = (back * up * (sig * (1.0 + gate * (1.0 - sig)))).astype(BF16)
        grads_ref[:, BLOCK:] = (back * silu).astype(BF16)
        act_ref[...] = act
        part = jnp.sum(act.astype(F32) * back, axis=1, keepdims=True)

        @pl.when(pl.program_id(0) == 0)
        def _():
            prob_ref[...] = part
            rows_out[...] = rows
            scaled_out[...] = scaled

        @pl.when(pl.program_id(0) > 0)
        def _():
            prob_ref[...] += part

    return pl.pallas_call(
        body,
        grid=(ff // BLOCK,),
        in_specs=[
            pl.BlockSpec((experts, 1, capacity, width), lambda j: (0, 0, 0, 0)),
            pl.BlockSpec((experts, 1, capacity, width), lambda j: (0, 1, 0, 0)),
            pl.BlockSpec((3, width, BLOCK), lambda j: (0, 0, j)),
        ],
        out_specs=[
            pl.BlockSpec((slots, 2 * BLOCK), lambda j: (0, j)),
            pl.BlockSpec((slots, BLOCK), lambda j: (0, j)),
            pl.BlockSpec((slots, 1), lambda j: (0, 0)),
            pl.BlockSpec((slots, width), lambda j: (0, 0)),
            pl.BlockSpec((slots, width), lambda j: (0, 0)),
        ],
        out_shape=[
            jax.ShapeDtypeStruct((slots, 2 * ff), BF16),
            jax.ShapeDtypeStruct((slots, ff), BF16),
            jax.ShapeDtypeStruct((slots, 1), F32),
            jax.ShapeDtypeStruct((slots, width), BF16),
            jax.ShapeDtypeStruct((slots, width), BF16),
        ],
        compiler_params=params(),
        name="hidden",
    )(received, received, weights)


def route_back(grads, weights, prob):
    slots, width, ff = grads.shape[0], *weights.shape[1:]
    steps = width // BLOCK

    def body(grads_ref, w_ref, prob_ref, out_ref):
        @pl.when(pl.program_id(0) < steps)
        def _():
            value = jnp.zeros((slots, BLOCK), F32)
            for j in range(ff // BLOCK):
                for n in range(2):
                    at = (2 * j + n) * BLOCK
                    value += dot_last(
                        grads_ref[:, at : at + BLOCK], w_ref[n, :, j * BLOCK : (j + 1) * BLOCK]
                    )
            out_ref[...] = value.astype(BF16)

        @pl.when(pl.program_id(0) == steps)
        def _():
            out_ref[...] = jnp.broadcast_to(prob_ref[...], (slots, BLOCK)).astype(BF16)

    return pl.pallas_call(
        body,
        grid=(steps + 1,),
        in_specs=[
            pl.BlockSpec((slots, 2 * ff), lambda i: (0, 0)),
            pl.BlockSpec((2, BLOCK, ff), lambda i: (0, jnp.minimum(i, steps - 1), 0)),
            pl.BlockSpec((slots, 1), lambda i: (0, 0)),
        ],
        out_specs=pl.BlockSpec((slots, BLOCK), lambda i: (0, i)),
        out_shape=jax.ShapeDtypeStruct((slots, width + BLOCK), BF16),
        compiler_params=params(),
        name="route_back",
    )(grads, weights, prob)


def per_device(
    tokens, out_grad, routes, route_probs, kept_count, gate_weight, up_weight, down_weight
):
    tok_rows, width = tokens.shape
    top = routes.shape[1]
    experts = lax.axis_size("expert")
    chips = lax.axis_size("dp") // 2
    capacity = 2 * tok_rows * top // experts
    slots = experts * capacity
    ff = gate_weight.shape[2]
    dp = lax.axis_index("dp")
    chip, core = dp // 2, dp % 2
    swap = [(2 * z + c, 2 * z + 1 - c) for z in range(chips) for c in range(2)]
    up_ring = [(2 * z + c, 2 * ((z + 1) % chips) + c) for z in range(chips) for c in range(2)]
    down_ring = [(2 * z + c, 2 * ((z - 1) % chips) + c) for z in range(chips) for c in range(2)]

    weights = lax.all_gather(
        jnp.concatenate((gate_weight, up_weight, down_weight), axis=0), "dp", axis=1, tiled=True
    )

    row = lax.axis_index("expert") * tok_rows + jnp.arange(tok_rows, dtype=jnp.int32)
    kept = row < kept_count[0]
    flat = routes.reshape(-1)
    onehot = (flat[:, None] == jnp.arange(experts, dtype=jnp.int32)[None, :]).astype(jnp.int32)
    before = jnp.cumsum(onehot, axis=0) - onehot
    position = jnp.sum(before * onehot, axis=1)
    target = (flat * capacity + position).reshape(tok_rows, top)
    probs = route_probs.astype(F32)
    factor = jnp.where(kept[:, None], probs, 0.0)
    line = jnp.arange(2 * slots, dtype=jnp.int32)[:, None]
    line_slot = line // (2 * capacity) * capacity + line % capacity
    line_half = line // capacity % 2
    twice = jnp.concatenate((target, target), axis=0)
    factor = jnp.concatenate((jnp.ones_like(probs), factor), axis=0)
    side = (jnp.arange(2 * tok_rows, dtype=jnp.int32) // tok_rows)[None, :]
    spread = sum(
        jnp.where((line_slot == twice[None, :, k]) & (line_half == side), factor[None, :, k], 0.0)
        for k in range(top)
    ).astype(BF16)
    send = dot(spread, jnp.concatenate((tokens, out_grad), axis=0)).astype(BF16)

    def exchange(value, lines):
        return lax.all_to_all(
            value.reshape(experts, lines, -1), "expert", split_axis=0, concat_axis=0, tiled=True
        )

    far = chips // 2
    at = [(chip + n) % chips for n in range(chips)]
    send, at, core, target = lax.optimization_barrier((send, at, core, target))
    received, at, core, target = lax.optimization_barrier(
        (exchange(send, 2 * capacity), at, core, target)
    )
    grads, act, prob_part, rows_in, scaled = hidden(
        received.reshape(experts, 2, capacity, width), weights
    )

    def add(*values):
        return sum(value.astype(F32) for value in values).astype(BF16)

    def block(part, n, side):
        return lax.dynamic_slice(part, (at[n], side, 0, 0), (1, 1, *part.shape[2:]))[0, 0]

    def half(part, side):
        return lax.dynamic_slice(part, (0, side, 0, 0), (chips, 1, *part.shape[2:]))[:, 0]

    down_part = dot_rows(scaled, act).astype(BF16).reshape(chips, 2, LANES, ff)
    down_other = lax.ppermute(half(down_part, 1 - core), "dp", swap)
    rows_in, down_part = lax.optimization_barrier((rows_in, down_part))
    gate_up = dot_rows(rows_in, grads).astype(BF16).reshape(chips, 2, LANES, 2 * ff)
    far_other = lax.ppermute(block(gate_up, far, 1 - core), "dp", swap)
    down_pair = add(half(down_part, core), down_other).reshape(chips * LANES, ff)
    gate_up, down_pair, far_other = lax.optimization_barrier((gate_up, down_pair, far_other))
    down_sum = lax.psum_scatter(
        down_pair,
        "dp",
        scatter_dimension=0,
        axis_index_groups=[[2 * z + c for z in range(chips)] for c in range(2)],
        tiled=True,
    )
    far_sum = add(block(gate_up, far, core), far_other)

    def both_ways(right, left):
        right, left = lax.optimization_barrier((right, left))
        right, left = lax.ppermute(right, "dp", up_ring), lax.ppermute(left, "dp", down_ring)
        return lax.optimization_barrier((right, left))

    def pair(n):
        return add(
            block(gate_up, n, core), lax.dynamic_slice(other, (at[n], 0, 0), (1, LANES, 2 * ff))[0]
        )

    grads, gate_up, far_sum = lax.optimization_barrier((grads, gate_up, far_sum))
    other = lax.ppermute(half(gate_up, 1 - core), "dp", swap)
    right, left = both_ways(far_sum[:, :ff], far_sum[:, ff:])
    back = route_back(grads, weights, prob_part)
    right, left, back = lax.optimization_barrier((right, left, back))
    zeros = jnp.zeros((LANES, ff), BF16)
    right = jnp.concatenate((right, zeros), axis=1)
    left = jnp.concatenate((zeros, left), axis=1)
    for n in range(far - 1, 0, -1):
        if n == 1:
            right, left, down_sum = lax.optimization_barrier((right, left, down_sum))
        right, left = both_ways(add(pair(n), right), add(pair(chips - n), left))
    back, right, left = lax.optimization_barrier((exchange(back, capacity), right, left))
    total = add(pair(0), right, left)
    columns = [
        total[:, (2 * j + n) * BLOCK : (2 * j + n + 1) * BLOCK]
        for n in range(2)
        for j in range(ff // BLOCK)
    ]
    weight_grad = jnp.concatenate((*columns, down_sum), axis=1)[None]

    back = back.reshape(slots, width + BLOCK)
    slot = jnp.arange(slots, dtype=jnp.int32)[:, None]
    match = [slot == target[None, :, k] for k in range(top)]
    placing = (match[0] | match[1]).astype(BF16)
    token_grad = dot_rows(placing, back[:, :width]).astype(BF16)
    prob_back = back[:, width].astype(F32)
    prob_grad = jnp.stack(
        [jnp.sum(jnp.where(m, prob_back[:, None], 0.0), axis=0) for m in match], axis=1
    )
    prob_grad = (prob_grad / probs).astype(BF16)
    return (token_grad, prob_grad, weight_grad)


def solution(mesh):
    in_specs = (
        P(("dp", "expert"), None),
        P(("dp", "expert"), None),
        P(("dp", "expert"), None),
        P(("dp", "expert"), None),
        P("dp"),
        P("expert", "dp", None),
        P("expert", "dp", None),
        P("expert", "dp", None),
    )
    out_specs = (P(("dp", "expert"), None), P(("dp", "expert"), None), P("expert", "dp", None))
    return jax.shard_map(
        per_device, mesh=mesh, in_specs=in_specs, out_specs=out_specs, check_vma=False
    )
```

time: 199 us -> 189 us (0.950)
  waiting for transfers between devices: 57.3 us -> 33.2 us
  matrix products: 37.2 us -> 15 us
  Pallas kernels: 0 us -> 21.5 us
  blocking collectives: 42.5 us -> 57.3 us
  local copies, waits for them, and re-layouts: 17.4 us -> 9.22 us
  other arithmetic: 8.16 us -> 16.3 us
    all_to_all x0 -> x1, blocking collectives: none -> 57.3 us  [exchange(): lax.all_to_all(value.reshape(experts, lines, -1), 'expert', split_axis=0,...]
    all_gather x1 -> x0, blocking collectives: 42.5 us -> none  [per_device(): lax.all_gather(prob_part.astype(jnp.bfloat16).reshape(experts, capacity),...]
    ppermute x0 -> x11, waiting for transfers between devices: none -> 31.7 us  [the longest x4 31.7 us: both_ways(): lax.ppermute(right, 'dp', up_ring)]
    all_to_all x3 -> x1, waiting for transfers between devices: 27.6 us -> 0.01 us  [exchange(): lax.all_to_all(value.reshape(experts, lines, -1), 'expert', split_axis=0,...]
    dot_general x11 -> x4, matrix products: 37.2 us -> 15 us  [the longest x3 12 us: dot_rows(): lax.dot_general(left, right, (((0,), (0,)), ((), ())), preferred_element_...]
    pallas_call x0 -> x2, Pallas kernels: none -> 21.5 us  [the longest x1 11.8 us: hidden(): pl.pallas_call(body, grid=(ff // BLOCK,), in_specs=[pl.BlockSpec((experts...]
    all_gather x1, waiting for transfers between devices: 19.1 us -> 1.45 us  [per_device(): lax.all_gather(jnp.concatenate((gate_weight, up_weight, down_weight), axi...]
    ppermute x0 -> x11, starting transfers between devices: none -> 15 us  [the longest x4 11.5 us: both_ways(): lax.ppermute(left, 'dp', down_ring)]
  transfers between devices with their start and end apart: 5 -> 14, of which waited for: 3 -> 4; matrix products, arithmetic and copies ran while one was open for 14% -> 11% of each run, Pallas kernels for 0% -> 5%
where the time goes in v2:
time: 189 us; the launch traced here: 187 us
  blocking collectives  57.3 us (30%)
  waiting for transfers between devices  33.2 us (18%)
  Pallas kernels  21.5 us (11%)
  starting transfers between devices  19.6 us (10%)
  other arithmetic  16.3 us (9%)
  between operations  15.1 us (8%)
  matrix products  15 us (8%)
  local copies, waits for them, and re-layouts  9.22 us (5%)
    all_to_all x1, blocking collectives, exchange(): lax.all_to_all(value.reshape(experts, lines, -1), 'expert', split_axis=0,...  57.3 us
    ppermute x4, waiting for transfers between devices, both_ways(): lax.ppermute(right, 'dp', up_ring)  31.7 us
    dot_general x3, matrix products, dot_rows(): lax.dot_general(left, right, (((0,), (0,)), ((), ())), preferred_element_...  12 us
    pallas_call x1, Pallas kernels, hidden(): pl.pallas_call(body, grid=(ff // BLOCK,), in_specs=[pl.BlockSpec((experts...  11.8 us
    ppermute x4, starting transfers between devices, both_ways(): lax.ppermute(left, 'dp', down_ring)  11.5 us
    convert_element_type x6, other arithmetic, add(): return sum((value.astype(F32) for value in values)).astype(BF16)  10.5 us
    pallas_call x1, Pallas kernels, route_back(): pl.pallas_call(body, grid=(steps + 1,), in_specs=[pl.BlockSpec((slots, 2...  9.68 us
    all_to_all x1, starting transfers between devices, exchange(): lax.all_to_all(value.reshape(experts, lines, -1), 'expert', split_axis=0,...  4.45 us
  transfers between devices with their start and end apart: 14, of which 4 were waited for; matrix products, arithmetic and copies ran while one was open for 11% of the time, Pallas kernels for 5%

profile of v2, /device:TPU:1, one launch (start us, length us, event | category | flops | bytes accessed | tf_op | source)
XLA Modules:
  0.0 187.2 jit_solution(12138935305377728794)
XLA Ops:
  7.2 2.0 %pad_maximum_fusion = bf16[3,128,768]{2,1,0:T(8,128)(2,1)} fusion(bf16[1,128,768]{2,1,0:T(8,128)(2,1)} %param.15, bf16[1,128,768]{2,1,0:T(8,128)(2,1)} %param.14, bf16[1,128,768]{2,1,0:T(8,128)(2,1)} %param.13), kind=kLoop, calls=%fused_computation.38 | loop fusion | flops 589824 | bytes 1179648 | tf_op jit(solution)/shard_map/concatenate | solution.py:140
  9.4 0.8 copy.36
  10.2 0.1 eq.130
  10.3 0.1 eq.126
  11.1 0.6 reduce-window.6
  11.7 0.2 slice_reduce_fusion
  12.0 0.1 fusion.27
  12.1 0.1 reduce_sum.30
  12.2 0.1 copy.39
  12.3 0.7 convert_select_fusion
  13.0 0.7 multiply_add_fusion
  13.7 3.0 %convolution_convert_fusion.1 = bf16[1024,2048]{1,0:T(8,128)(2,1)S(1)} fusion(bf16[128,2048]{1,0:T(8,128)(2,1)} %param.9, bf16[128,2048]{1,0:T(8,128)(2,1)} %param.8, f32[256]{0:T(256)S(1)} %bitcast.115, s32[256]{0:T(256)S(1)} %bitcast.117, f32[256]{0:T(256)S(1)} %bitcast.114, s32[256]{0:T(256)S(1)} %and_select_fusion, s32[256]{0:T(256)S(1)} %bitcast.116, ...), kind=kOutput, calls=%fused_computation.1 | convolution fusion | flops 1080295424 | bytes 5256192 | tf_op jit(solution)/shard_map/dot_general | solution.py:16
  16.7 57.3 %all_to_all.10 = bf16[16,64,2048]{2,1,0:T(8,128)(2,1)} all-to-all(bf16[16,64,2048]{2,1,0:T(8,128)(2,1)S(1)} %bitcast.108), channel_id=1, replica_groups=mesh['dp'=16,'expert'=16] {'expert'}, dimensions={0} | all-to-all | bytes 8388608 | tf_op jit(solution)/shard_map/all_to_all | solution.py:165
  74.1 1.4 all-gather.2.cloned.1.call-done.w_ref
  75.5 11.8 %hidden.1 = (bf16[512,1536]{1,0:T(8,128)(2,1)}, bf16[512,768]{1,0:T(8,128)(2,1)}, f32[512,1]{1,0:T(8,128)}, bf16[512,2048]{1,0:T(8,128)(2,1)}, bf16[512,2048]{1,0:T(8,128)(2,1)}) custom-call(bf16[16,2,32,2048]{3,2,1,0:T(8,128)(2,1)} %bitcast.97, bf16[16,2,32,2048]{3,2,1,0:T(8,128)(2,1)} %bitcast.98, bf16[3,2048,768]{2,1,0:T(8,128)(2,1)} %all-gather.2.cloned.1.call-done.w_ref), custom_call_target="tpu_custom_call" | custom-call | tf_op jit(solution)/shard_map/hidden/pallas_call | solution.py:61
  87.4 3.6 %convolution_convert_fusion.2 = bf16[2048,768]{1,0:T(8,128)(2,1)S(1)} fusion(bf16[512,2048]{1,0:T(8,128)(2,1)} %get-tuple-element.78, bf16[512,768]{1,0:T(8,128)(2,1)} %get-tuple-element.79), kind=kOutput, calls=%fused_computation.2 | convolution fusion | flops 1612185600 | bytes 6029312 | tf_op jit(solution)/shard_map/dot_general | solution.py:20
  91.0 1.3 dynamic-slice_bitcast_fusion.1
  92.3 0.5 collective-permute-start
  92.8 5.5 %convolution_convert_fusion = bf16[2048,1536]{1,0:T(8,128)(2,1)S(1)} fusion(bf16[512,2048]{1,0:T(8,128)(2,1)} %get-tuple-element.80, bf16[512,1536]{1,0:T(8,128)(2,1)} %get-tuple-element.91.grads_ref), kind=kOutput, calls=%fused_computation | convolution fusion | flops 3224371200 | bytes 9961472 | tf_op jit(solution)/shard_map/dot_general | solution.py:20
  98.3 2.7 %copy-done = bf16[2048,1536]{1,0:T(8,128)(2,1)} copy-done((bf16[2048,1536]{1,0:T(8,128)(2,1)}, bf16[2048,1536]{1,0:T(8,128)(2,1)S(1)}, u32[]{:S(2)}) %copy-start) | copy-done | bytes 6291480
  101.0 0.1 collective-permute-start.1
  101.2 3.0 %fusion = bf16[8,128,768]{2,1,0:T(8,128)(2,1)} fusion(bf16[8,128,768]{2,1,0:T(8,128)(2,1)} %collective-permute-done, bf16[8,2,128,768]{3,2,1,0:T(8,128)(2,1)S(1)} %bitcast.110, s32[]{:T(128)S(6)} %select_n.184), kind=kLoop, calls=%fused_computation.4 | loop fusion | flops 3145728 | bytes 4718596 | tf_op jit(solution)/shard_map/convert_element_type | solution.py:180
  104.2 1.2 fusion.12
  105.4 2.1 %dynamic-slice_bitcast_fusion = bf16[8,128,1536]{2,1,0:T(8,128)(2,1)S(1)} fusion(bf16[8,2,128,1536]{3,2,1,0:T(8,128)(2,1)} %bitcast.102, s32[]{:T(128)S(6)} %select_n.185), kind=kLoop, calls=%fused_computation.5 | loop fusion | bytes 6291460 | tf_op jit(solution)/shard_map/squeeze | solution.py:186
  107.5 0.6 collective-permute-start.4
  108.1 0.8 fusion.45
  108.8 1.7 collective-permute-start.2
  110.5 3.9 %collective-permute-start.3 = (bf16[128,768]{1,0:T(8,128)(2,1)}, bf16[128,768]{1,0:T(8,128)(2,1)S(1)}, u32[]{:S(2)}, u32[]{:S(2)}) collective-permute-start(bf16[128,768]{1,0:T(8,128)(2,1)} %get-tuple-element.88), channel_id=1, source_target_pairs={{0,224},{16,240},{32,0},{48,16},{64,32},{80,48},{96,64},{112,80},{... | collective-permute-start | bytes 589832 | tf_op jit(solution)/shard_map/ppermute | solution.py:206
  114.4 9.7 %route_back.1 = bf16[512,2304]{1,0:T(8,128)(2,1)} custom-call(bf16[512,1536]{1,0:T(8,128)(2,1)} %get-tuple-element.91.grads_ref, bf16[3,2048,768]{2,1,0:T(8,128)(2,1)} %all-gather.2.cloned.1.call-done.w_ref, f32[512,1]{1,0:T(8,128)} %get-tuple-element.92.prob_ref), custom_call_target="tpu_custom_call" | custom-call | tf_op jit(solution)/shard_map/route_back/pallas_call | solution.py:108
  124.1 4.4 %all-to-all-start.1 = ((bf16[16,32,2304]{2,1,0:T(8,128)(2,1)}), bf16[16,32,2304]{2,1,0:T(8,128)(2,1)}, u32[]{:S(2)}, u32[]{:S(2)}) async-start(bf16[16,32,2304]{2,1,0:T(8,128)(2,1)} %bitcast.99), calls=%async_computation.1 | async-start | bytes 4718592 | tf_op jit(solution)/shard_map/all_to_all | solution.py:165
  128.6 1.6 add_convert_fusion.6
  130.2 0.1 collective-permute-start.5
  130.3 2.7 %collective-permute-start.6 = (bf16[128,1536]{1,0:T(8,128)(2,1)S(1)}, bf16[128,1536]{1,0:T(8,128)(2,1)S(1)}, u32[]{:S(2)}, u32[]{:S(2)}) collective-permute-start(bf16[128,1536]{1,0:T(8,128)(2,1)S(1)} %get-tuple-element.102), channel_id=1, source_target_pairs={{0,224},{16,240},{32,0},{48,16},{64,32},{80,48},{96,64},{112,80},{... | collective-permute-start | bytes 1179656 | tf_op jit(solution)/shard_map/ppermute | solution.py:206
  133.0 15.5 %collective-permute-done.5 = bf16[128,1536]{1,0:T(8,128)(2,1)S(1)} collective-permute-done((bf16[128,1536]{1,0:T(8,128)(2,1)S(1)}, bf16[128,1536]{1,0:T(8,128)(2,1)S(1)}, u32[]{:S(2)}, u32[]{:S(2)}) %collective-permute-start.5) | collective-permute-done | bytes 393248 | tf_op jit(solution)/shard_map/ppermute | solution.py:206
  148.5 1.6 add_convert_fusion.4
  150.2 0.1 collective-permute-start.7
  150.3 2.7 %collective-permute-start.8 = (bf16[128,1536]{1,0:T(8,128)(2,1)S(1)}, bf16[128,1536]{1,0:T(8,128)(2,1)S(1)}, u32[]{:S(2)}, u32[]{:S(2)}) collective-permute-start(bf16[128,1536]{1,0:T(8,128)(2,1)S(1)} %get-tuple-element.107), channel_id=1, source_target_pairs={{0,224},{16,240},{32,0},{48,16},{64,32},{80,48},{96,64},{112,80},{... | collective-permute-start | bytes 1179656 | tf_op jit(solution)/shard_map/ppermute | solution.py:206
  152.9 8.5 %collective-permute-done.7 = bf16[128,1536]{1,0:T(8,128)(2,1)S(1)} collective-permute-done((bf16[128,1536]{1,0:T(8,128)(2,1)S(1)}, bf16[128,1536]{1,0:T(8,128)(2,1)S(1)}, u32[]{:S(2)}, u32[]{:S(2)}) %collective-permute-start.7) | collective-permute-done | bytes 393248 | tf_op jit(solution)/shard_map/ppermute | solution.py:206
  161.5 1.6 add_convert_fusion.2
  163.2 0.6 collective-permute-start.9
  163.7 2.2 %collective-permute-start.10 = (bf16[128,1536]{1,0:T(8,128)(2,1)S(1)}, bf16[128,1536]{1,0:T(8,128)(2,1)S(1)}, u32[]{:S(2)}, u32[]{:S(2)}) collective-permute-start(bf16[128,1536]{1,0:T(8,128)(2,1)S(1)} %get-tuple-element.115), channel_id=1, source_target_pairs={{0,224},{16,240},{32,0},{48,16},{64,32},{80,48},{96,64},{112,80},{... | collective-permute-start | bytes 1179656 | tf_op jit(solution)/shard_map/ppermute | solution.py:206
  165.9 7.6 %collective-permute-done.9 = bf16[128,1536]{1,0:T(8,128)(2,1)S(1)} collective-permute-done((bf16[128,1536]{1,0:T(8,128)(2,1)S(1)}, bf16[128,1536]{1,0:T(8,128)(2,1)S(1)}, u32[]{:S(2)}, u32[]{:S(2)}) %collective-permute-start.9) | collective-permute-done | bytes 393248 | tf_op jit(solution)/shard_map/ppermute | solution.py:206
  173.5 1.0 convert_reduce_fusion
  174.6 2.9 %convolution_convert_fusion.3 = bf16[128,2048]{1,0:T(8,128)(2,1)} fusion(bf16[512,2304]{1,0:T(8,128)(2,1)} %bitcast.31, s32[128]{0:T(128)S(1)} %get-tuple-element.134, s32[128]{0:T(128)S(1)} %get-tuple-element.133), kind=kOutput, calls=%fused_computation.6 | convolution fusion | flops 268894208 | bytes 2622464 | tf_op jit(solution)/shard_map/dot_general | solution.py:20
  177.4 0.1 select_reduce_fusion.1
  177.6 1.4 add_convert_fusion.1
  179.0 0.5 fusion.42
  179.6 0.8 copy-done.2
  (37 shorter events, 0.3 us)
Async XLA Ops:
  7.2 68.4 %all-gather.2.cloned.1.call-start = ((), (), s32[]{:S(2)}) async-start(), calls=%async_computation.3 | async-start | bytes 10027008 | tf_op jit(solution)/shard_map/all_gather | solution.py:139
  9.2 152.3 %reduce-scatter.2.cloned.1.call-start = ((), (), s32[]{:S(2)}) async-start(), calls=%async_computation.4 | async-start | bytes 1769472 | tf_op jit(solution)/shard_map/reduce_scatter | solution.py:195
  92.3 8.9 %collective-permute-start = (bf16[8,128,768]{2,1,0:T(8,128)(2,1)}, bf16[8,128,768]{2,1,0:T(8,128)(2,1)}, u32[]{:S(2)}, u32[]{:S(2)}) collective-permute-start(bf16[8,128,768]{2,1,0:T(8,128)(2,1)} %dynamic-slice_bitcast_fusion.1), channel_id=1, source_target_pairs={{0,16},{16,0},{32,48},{48,32},{64,80},{80,64},{96,112},{112,96},{1... | collective-permute-start | bytes 4718600 | tf_op jit(solution)/shard_map/ppermute | solution.py:189
  98.3 2.7 %copy-start = (bf16[2048,1536]{1,0:T(8,128)(2,1)}, bf16[2048,1536]{1,0:T(8,128)(2,1)S(1)}, u32[]{:S(2)}) copy-start(bf16[2048,1536]{1,0:T(8,128)(2,1)S(1)} %convolution_convert_fusion) | copy-start | bytes 18874372
  101.0 3.1 %collective-permute-start.1 = (bf16[128,1536]{1,0:T(8,128)(2,1)S(1)}, bf16[128,1536]{1,0:T(8,128)(2,1)}, u32[]{:S(2)}, u32[]{:S(2)}) collective-permute-start(bf16[128,1536]{1,0:T(8,128)(2,1)S(1)} %dynamic-slice_bitcast_fusion.2), channel_id=1, source_target_pairs={{0,16},{16,0},{32,48},{48,32},{64,80},{80,64},{96,112},{112,96},{1... | collective-permute-start | bytes 1179656 | tf_op jit(solution)/shard_map/ppermute | solution.py:192
  107.5 21.1 %collective-permute-start.4 = (bf16[8,128,1536]{2,1,0:T(8,128)(2,1)S(1)}, bf16[8,128,1536]{2,1,0:T(8,128)(2,1)}, u32[]{:S(2)}, u32[]{:S(2)}) collective-permute-start(bf16[8,128,1536]{2,1,0:T(8,128)(2,1)S(1)} %dynamic-slice_bitcast_fusion), channel_id=1, source_target_pairs={{0,16},{16,0},{32,48},{48,32},{64,80},{80,64},{96,112},{112,96},{1... | collective-permute-start | bytes 9437192 | tf_op jit(solution)/shard_map/ppermute | solution.py:215
  108.8 15.3 %collective-permute-start.2 = (bf16[128,768]{1,0:T(8,128)(2,1)}, bf16[128,768]{1,0:T(8,128)(2,1)S(1)}, u32[]{:S(2)}, u32[]{:S(2)}) collective-permute-start(bf16[128,768]{1,0:T(8,128)(2,1)} %get-tuple-element.87), channel_id=1, source_target_pairs={{0,32},{16,48},{32,64},{48,80},{64,96},{80,112},{96,128},{112,144}... | collective-permute-start | bytes 589832 | tf_op jit(solution)/shard_map/ppermute | solution.py:206
  110.5 13.6 %collective-permute-start.3 = (bf16[128,768]{1,0:T(8,128)(2,1)}, bf16[128,768]{1,0:T(8,128)(2,1)S(1)}, u32[]{:S(2)}, u32[]{:S(2)}) collective-permute-start(bf16[128,768]{1,0:T(8,128)(2,1)} %get-tuple-element.88), channel_id=1, source_target_pairs={{0,224},{16,240},{32,0},{48,16},{64,32},{80,48},{96,64},{112,80},{... | collective-permute-start | bytes 589832 | tf_op jit(solution)/shard_map/ppermute | solution.py:206
  124.1 49.4 %all-to-all-start.1 = ((bf16[16,32,2304]{2,1,0:T(8,128)(2,1)}), bf16[16,32,2304]{2,1,0:T(8,128)(2,1)}, u32[]{:S(2)}, u32[]{:S(2)}) async-start(bf16[16,32,2304]{2,1,0:T(8,128)(2,1)} %bitcast.99), calls=%async_computation.1 | async-start | bytes 4718592 | tf_op jit(solution)/shard_map/all_to_all | solution.py:165
  130.2 18.3 %collective-permute-start.5 = (bf16[128,1536]{1,0:T(8,128)(2,1)S(1)}, bf16[128,1536]{1,0:T(8,128)(2,1)S(1)}, u32[]{:S(2)}, u32[]{:S(2)}) collective-permute-start(bf16[128,1536]{1,0:T(8,128)(2,1)S(1)} %get-tuple-element.101), channel_id=1, source_target_pairs={{0,32},{16,48},{32,64},{48,80},{64,96},{80,112},{96,128},{112,144}... | collective-permute-start | bytes 1179656 | tf_op jit(solution)/shard_map/ppermute | solution.py:206
  130.3 18.2 %collective-permute-start.6 = (bf16[128,1536]{1,0:T(8,128)(2,1)S(1)}, bf16[128,1536]{1,0:T(8,128)(2,1)S(1)}, u32[]{:S(2)}, u32[]{:S(2)}) collective-permute-start(bf16[128,1536]{1,0:T(8,128)(2,1)S(1)} %get-tuple-element.102), channel_id=1, source_target_pairs={{0,224},{16,240},{32,0},{48,16},{64,32},{80,48},{96,64},{112,80},{... | collective-permute-start | bytes 1179656 | tf_op jit(solution)/shard_map/ppermute | solution.py:206
  150.2 11.3 %collective-permute-start.7 = (bf16[128,1536]{1,0:T(8,128)(2,1)S(1)}, bf16[128,1536]{1,0:T(8,128)(2,1)S(1)}, u32[]{:S(2)}, u32[]{:S(2)}) collective-permute-start(bf16[128,1536]{1,0:T(8,128)(2,1)S(1)} %get-tuple-element.106), channel_id=1, source_target_pairs={{0,32},{16,48},{32,64},{48,80},{64,96},{80,112},{96,128},{112,144}... | collective-permute-start | bytes 1179656 | tf_op jit(solution)/shard_map/ppermute | solution.py:206
  150.3 11.2 %collective-permute-start.8 = (bf16[128,1536]{1,0:T(8,128)(2,1)S(1)}, bf16[128,1536]{1,0:T(8,128)(2,1)S(1)}, u32[]{:S(2)}, u32[]{:S(2)}) collective-permute-start(bf16[128,1536]{1,0:T(8,128)(2,1)S(1)} %get-tuple-element.107), channel_id=1, source_target_pairs={{0,224},{16,240},{32,0},{48,16},{64,32},{80,48},{96,64},{112,80},{... | collective-permute-start | bytes 1179656 | tf_op jit(solution)/shard_map/ppermute | solution.py:206
  163.1 15.9 %copy-start.3 = (bf16[128,2]{0,1:T(2,128)(2,1)S(1)}, bf16[128,2]{0,1:T(2,128)(2,1)}, u32[]{:S(2)}) copy-start(bf16[128,2]{0,1:T(2,128)(2,1)} %param.11) | copy-start | bytes 1540
  163.1 16.4 %copy-start.1 = (bf16[128,768]{1,0:T(8,128)(2,1)S(1)}, bf16[128,768]{1,0:T(8,128)(2,1)}, u32[]{:S(2)}) copy-start(bf16[128,768]{1,0:T(8,128)(2,1)} %reduce-scatter.2.cloned.1.call-done) | copy-start | bytes 589828
  163.2 10.4 %collective-permute-start.9 = (bf16[128,1536]{1,0:T(8,128)(2,1)S(1)}, bf16[128,1536]{1,0:T(8,128)(2,1)S(1)}, u32[]{:S(2)}, u32[]{:S(2)}) collective-permute-start(bf16[128,1536]{1,0:T(8,128)(2,1)S(1)} %get-tuple-element.114), channel_id=1, source_target_pairs={{0,32},{16,48},{32,64},{48,80},{64,96},{80,112},{96,128},{112,144}... | collective-permute-start | bytes 1179656 | tf_op jit(solution)/shard_map/ppermute | solution.py:206
  163.7 9.8 %collective-permute-start.10 = (bf16[128,1536]{1,0:T(8,128)(2,1)S(1)}, bf16[128,1536]{1,0:T(8,128)(2,1)S(1)}, u32[]{:S(2)}, u32[]{:S(2)}) collective-permute-start(bf16[128,1536]{1,0:T(8,128)(2,1)S(1)} %get-tuple-element.115), channel_id=1, source_target_pairs={{0,224},{16,240},{32,0},{48,16},{64,32},{80,48},{96,64},{112,80},{... | collective-permute-start | bytes 1179656 | tf_op jit(solution)/shard_map/ppermute | solution.py:206
  179.6 0.8 copy-start.2
Sparse Core Ops, SparseCore 0:
  10.4 65.0 all-gather.1
  108.2 37.9 reduce-scatter.1

commit v3 on v2

--- a/solution.py
+++ b/solution.py
@@ -30,11 +30,11 @@
     )
 
 
-def hidden(received, weights):
+def hidden(received, weights, core):
     experts, _, capacity, width = received.shape
     slots, ff = experts * capacity, weights.shape[2]
 
-    def body(rows_ref, scaled_ref, w_ref, grads_ref, act_ref, prob_ref, rows_out, scaled_out):
+    def body(s_ref, rows_ref, scaled_ref, w_ref, grads_ref, act_ref, prob_ref, *apart):
         rows = rows_ref[...].reshape(slots, width)
         scaled = scaled_ref[...].reshape(slots, width)
         gate = dot(rows, w_ref[0])
@@ -43,16 +43,29 @@
         sig = jax.nn.sigmoid(gate)
         silu = gate * sig
         act = (silu * up).astype(BF16)
-        grads_ref[:, :BLOCK] = (back * up * (sig * (1.0 + gate * (1.0 - sig)))).astype(BF16)
-        grads_ref[:, BLOCK:] = (back * silu).astype(BF16)
+        d_gate = (back * up * (sig * (1.0 + gate * (1.0 - sig)))).astype(BF16)
+        d_up = (back * silu).astype(BF16)
+        for j in range(ff // BLOCK):
+
+            @pl.when(pl.program_id(0) == j)
+            def _():
+                grads_ref[:, j * BLOCK : (j + 1) * BLOCK] = d_gate
+                grads_ref[:, ff + j * BLOCK : ff + (j + 1) * BLOCK] = d_up
+
         act_ref[...] = act
         part = jnp.sum(act.astype(F32) * back, axis=1, keepdims=True)
 
         @pl.when(pl.program_id(0) == 0)
         def _():
             prob_ref[...] = part
-            rows_out[...] = rows
-            scaled_out[...] = scaled
+            first = s_ref[0] == 0
+            for value, own_ref, other_ref in ((rows, *apart[:2]), (scaled, *apart[2:])):
+                for n in range(width // (2 * LANES)):
+                    at = slice(n * LANES, (n + 1) * LANES)
+                    low = value[:, 2 * n * LANES : (2 * n + 1) * LANES]
+                    high = value[:, (2 * n + 1) * LANES : (2 * n + 2) * LANES]
+                    own_ref[:, at] = jnp.where(first, low, high)
+                    other_ref[:, at] = jnp.where(first, high, low)
 
         @pl.when(pl.program_id(0) > 0)
         def _():
@@ -60,29 +73,30 @@
 
     return pl.pallas_call(
         body,
-        grid=(ff // BLOCK,),
-        in_specs=[
-            pl.BlockSpec((experts, 1, capacity, width), lambda j: (0, 0, 0, 0)),
-            pl.BlockSpec((experts, 1, capacity, width), lambda j: (0, 1, 0, 0)),
-            pl.BlockSpec((3, width, BLOCK), lambda j: (0, 0, j)),
-        ],
-        out_specs=[
-            pl.BlockSpec((slots, 2 * BLOCK), lambda j: (0, j)),
-            pl.BlockSpec((slots, BLOCK), lambda j: (0, j)),
-            pl.BlockSpec((slots, 1), lambda j: (0, 0)),
-            pl.BlockSpec((slots, width), lambda j: (0, 0)),
-            pl.BlockSpec((slots, width), lambda j: (0, 0)),
-        ],
+        grid_spec=pltpu.PrefetchScalarGridSpec(
+            num_scalar_prefetch=1,
+            grid=(ff // BLOCK,),
+            in_specs=[
+                pl.BlockSpec((experts, 1, capacity, width), lambda j, s: (0, 0, 0, 0)),
+                pl.BlockSpec((experts, 1, capacity, width), lambda j, s: (0, 1, 0, 0)),
+                pl.BlockSpec((3, width, BLOCK), lambda j, s: (0, 0, j)),
+            ],
+            out_specs=[
+                pl.BlockSpec((slots, 2 * ff), lambda j, s: (0, 0)),
+                pl.BlockSpec((slots, BLOCK), lambda j, s: (0, j)),
+                pl.BlockSpec((slots, 1), lambda j, s: (0, 0)),
+            ]
+            + [pl.BlockSpec((slots, width // 2), lambda j, s: (0, 0))] * 4,
+        ),
         out_shape=[
             jax.ShapeDtypeStruct((slots, 2 * ff), BF16),
             jax.ShapeDtypeStruct((slots, ff), BF16),
             jax.ShapeDtypeStruct((slots, 1), F32),
-            jax.ShapeDtypeStruct((slots, width), BF16),
-            jax.ShapeDtypeStruct((slots, width), BF16),
-        ],
+        ]
+        + [jax.ShapeDtypeStruct((slots, width // 2), BF16)] * 4,
         compiler_params=params(),
         name="hidden",
-    )(received, received, weights)
+    )(core[None].astype(jnp.int32), received, received, weights)
 
 
 def route_back(grads, weights, prob):
@@ -92,13 +106,7 @@
     def body(grads_ref, w_ref, prob_ref, out_ref):
         @pl.when(pl.program_id(0) < steps)
         def _():
-            value = jnp.zeros((slots, BLOCK), F32)
-            for j in range(ff // BLOCK):
-                for n in range(2):
-                    at = (2 * j + n) * BLOCK
-                    value += dot_last(
-                        grads_ref[:, at : at + BLOCK], w_ref[n, :, j * BLOCK : (j + 1) * BLOCK]
-                    )
+            value = dot_last(grads_ref[:, :ff], w_ref[0]) + dot_last(grads_ref[:, ff:], w_ref[1])
             out_ref[...] = value.astype(BF16)
 
         @pl.when(pl.program_id(0) == steps)
@@ -172,65 +180,68 @@
     received, at, core, target = lax.optimization_barrier(
         (exchange(send, 2 * capacity), at, core, target)
     )
-    grads, act, prob_part, rows_in, scaled = hidden(
-        received.reshape(experts, 2, capacity, width), weights
+    grads, act, prob_part, rows_own, rows_other, scaled_own, scaled_other = hidden(
+        received.reshape(experts, 2, capacity, width), weights, core
     )
 
     def add(*values):
         return sum(value.astype(F32) for value in values).astype(BF16)
 
-    def block(part, n, side):
-        return lax.dynamic_slice(part, (at[n], side, 0, 0), (1, 1, *part.shape[2:]))[0, 0]
-
-    def half(part, side):
-        return lax.dynamic_slice(part, (0, side, 0, 0), (chips, 1, *part.shape[2:]))[:, 0]
-
-    down_part = dot_rows(scaled, act).astype(BF16).reshape(chips, 2, LANES, ff)
-    down_other = lax.ppermute(half(down_part, 1 - core), "dp", swap)
-    rows_in, down_part = lax.optimization_barrier((rows_in, down_part))
-    gate_up = dot_rows(rows_in, grads).astype(BF16).reshape(chips, 2, LANES, 2 * ff)
-    far_other = lax.ppermute(block(gate_up, far, 1 - core), "dp", swap)
-    down_pair = add(half(down_part, core), down_other).reshape(chips * LANES, ff)
-    gate_up, down_pair, far_other = lax.optimization_barrier((gate_up, down_pair, far_other))
-    down_sum = lax.psum_scatter(
-        down_pair,
+    def swapped(value):
+        return lax.ppermute(value, "dp", swap)
+
+    def grad_of(left, right):
+        return dot_rows(left, right).astype(BF16)
+
+    def both_ways(right, left):
+        right, left = lax.optimization_barrier((right, left))
+        right, left = lax.ppermute(right, "dp", up_ring), lax.ppermute(left, "dp", down_ring)
+        return lax.optimization_barrier((right, left))
+
+    gate_up_other = swapped(grad_of(rows_other, grads))
+    far_own, far_other = (
+        grad_of(lax.dynamic_slice(lines, (0, at[far] * LANES), (slots, LANES)), act)
+        for lines in (scaled_own, scaled_other)
+    )
+    far_other = swapped(far_other)
+    other = swapped(grad_of(scaled_other, act))
+    gate_up_own = grad_of(rows_own, grads)
+    gate_up_own, gate_up_other, far_own, far_other, other = lax.optimization_barrier(
+        (gate_up_own, gate_up_other, far_own, far_other, other)
+    )
+    gate_up_pair = add(gate_up_own, gate_up_other)
+    far_sum = add(far_own, far_other)
+    gate_up_pair, far_sum, scaled_own, grads = lax.optimization_barrier(
+        (gate_up_pair, far_sum, scaled_own, grads)
+    )
+    gate_up_sum = lax.psum_scatter(
+        gate_up_pair,
         "dp",
         scatter_dimension=0,
         axis_index_groups=[[2 * z + c for z in range(chips)] for c in range(2)],
         tiled=True,
     )
-    far_sum = add(block(gate_up, far, core), far_other)
-
-    def both_ways(right, left):
-        right, left = lax.optimization_barrier((right, left))
-        right, left = lax.ppermute(right, "dp", up_ring), lax.ppermute(left, "dp", down_ring)
-        return lax.optimization_barrier((right, left))
-
-    def pair(n):
-        return add(
-            block(gate_up, n, core), lax.dynamic_slice(other, (at[n], 0, 0), (1, LANES, 2 * ff))[0]
-        )
-
-    grads, gate_up, far_sum = lax.optimization_barrier((grads, gate_up, far_sum))
-    other = lax.ppermute(half(gate_up, 1 - core), "dp", swap)
-    right, left = both_ways(far_sum[:, :ff], far_sum[:, ff:])
+    right, left = both_ways(far_sum[: LANES // 2], far_sum[LANES // 2 :])
+    own = grad_of(scaled_own, act)
     back = route_back(grads, weights, prob_part)
     right, left, back = lax.optimization_barrier((right, left, back))
-    zeros = jnp.zeros((LANES, ff), BF16)
-    right = jnp.concatenate((right, zeros), axis=1)
-    left = jnp.concatenate((zeros, left), axis=1)
+
+    def pair(n):
+        where, size = (at[n] * LANES, 0), (LANES, ff)
+        return add(lax.dynamic_slice(own, where, size), lax.dynamic_slice(other, where, size))
+
+    zeros = jnp.zeros((LANES // 2, ff), BF16)
+    right = jnp.concatenate((right, zeros), axis=0)
+    left = jnp.concatenate((zeros, left), axis=0)
     for n in range(far - 1, 0, -1):
-        if n == 1:
-            right, left, down_sum = lax.optimization_barrier((right, left, down_sum))
-        right, left = both_ways(add(pair(n), right), add(pair(chips - n), left))
-    back, right, left = lax.optimization_barrier((exchange(back, capacity), right, left))
-    total = add(pair(0), right, left)
-    columns = [
-        total[:, (2 * j + n) * BLOCK : (2 * j + n + 1) * BLOCK]
-        for n in range(2)
-        for j in range(ff // BLOCK)
-    ]
-    weight_grad = jnp.concatenate((*columns, down_sum), axis=1)[None]
+        right, left = add(pair(n), right), add(pair(chips - n), left)
+        if n == far - 1:
+            right, left, back = lax.optimization_barrier((right, left, back))
+            back = exchange(back, capacity)
+        right, left = both_ways(right, left)
+    down_sum = add(pair(0), right, left)
+    down_sum, gate_up_sum = lax.optimization_barrier((down_sum, gate_up_sum))
+    weight_grad = jnp.concatenate((gate_up_sum, down_sum), axis=1)[None]
 
     back = back.reshape(slots, width + BLOCK)
     slot = jnp.arange(slots, dtype=jnp.int32)[:, None]

time: 189 us -> 178 us (0.942)
  local copies, waits for them, and re-layouts: 9.22 us -> 1.52 us
  waiting for transfers between devices: 33.2 us -> 27.9 us
  other arithmetic: 16.3 us -> 13 us
  matrix products: 15 us -> 18 us
  Pallas kernels: 21.5 us -> 23.5 us
    ppermute x4, waiting for transfers between devices: 31.7 us -> 21.4 us  [both_ways(): lax.ppermute(right, 'dp', up_ring)]
    dot_general x3 -> x7, matrix products: 12 us -> 16.1 us  [dot_rows(): lax.dot_general(left, right, (((0,), (0,)), ((), ())), preferred_element_...]
    unnamed x15 -> x21, local copies, waits for them, and re-layouts: 4.32 us -> 0.83 us
    squeeze x3 -> x0, local copies, waits for them, and re-layouts: 3.43 us -> none  [the longest x2 3.41 us: half(): lax.dynamic_slice(part, (0, side, 0, 0), (chips, 1, *part.shape[2:]))[:, 0]]
    convert_element_type x6, other arithmetic: 10.5 us -> 7.55 us  [add(): return sum((value.astype(F32) for value in values)).astype(BF16)]
    ppermute x4, waiting for transfers between devices: 0.01 us -> 2.62 us  [both_ways(): lax.ppermute(left, 'dp', down_ring)]
    all_gather x1, waiting for transfers between devices: 1.45 us -> 3.82 us  [per_device(): lax.all_gather(jnp.concatenate((gate_weight, up_weight, down_weight), axi...]
    ppermute x4, starting transfers between devices: 2.39 us -> 0.25 us  [both_ways(): lax.ppermute(right, 'dp', up_ring)]
  transfers between devices with their start and end apart: 14 -> 14, of which waited for: 4 -> 5; matrix products, arithmetic and copies ran while one was open for 11% -> 12% of each run, Pallas kernels for 5% -> 6%
where the time goes in v3:
time: 178 us; the launch traced here: 175 us
  blocking collectives  57.3 us (32%)
  waiting for transfers between devices  27.9 us (16%)
  Pallas kernels  23.5 us (13%)
  starting transfers between devices  18.9 us (11%)
  matrix products  18 us (10%)
  between operations  15.3 us (9%)
  other arithmetic  13 us (7%)
    all_to_all x1, blocking collectives, exchange(): lax.all_to_all(value.reshape(experts, lines, -1), 'expert', split_axis=0,...  57.3 us
    ppermute x4, waiting for transfers between devices, both_ways(): lax.ppermute(right, 'dp', up_ring)  21.4 us
    dot_general x7, matrix products, dot_rows(): lax.dot_general(left, right, (((0,), (0,)), ((), ())), preferred_element_...  16.1 us
    pallas_call x1, Pallas kernels, hidden(): pl.pallas_call(body, grid_spec=pltpu.PrefetchScalarGridSpec(num_scalar_pr...  13.4 us
    ppermute x4, starting transfers between devices, both_ways(): lax.ppermute(left, 'dp', down_ring)  11.8 us
    pallas_call x1, Pallas kernels, route_back(): pl.pallas_call(body, grid=(steps + 1,), in_specs=[pl.BlockSpec((slots, 2...  10.2 us
    convert_element_type x6, other arithmetic, add(): return sum((value.astype(F32) for value in values)).astype(BF16)  7.55 us
    all_to_all x1, starting transfers between devices, exchange(): lax.all_to_all(value.reshape(experts, lines, -1), 'expert', split_axis=0,...  5.74 us
  transfers between devices with their start and end apart: 14, of which 5 were waited for; matrix products, arithmetic and copies ran while one was open for 12% of the time, Pallas kernels for 6%

profile of v3, /device:TPU:1, one launch (start us, length us, event | category | flops | bytes accessed | tf_op | source)
XLA Modules:
  0.0 175.4 jit_solution(4591792531533590183)
XLA Ops:
  7.2 0.0 all-gather.2.cloned.1.call-start
  7.3 2.1 %pad_maximum_fusion = bf16[3,128,768]{2,1,0:T(8,128)(2,1)} fusion(bf16[1,128,768]{2,1,0:T(8,128)(2,1)} %param.15, bf16[1,128,768]{2,1,0:T(8,128)(2,1)} %param.14, bf16[1,128,768]{2,1,0:T(8,128)(2,1)} %param.13), kind=kLoop, calls=%fused_computation.16 | loop fusion | flops 589824 | bytes 1179648 | tf_op jit(solution)/shard_map/concatenate | solution.py:148
  9.3 0.0 all-gather.2.cloned.1.call-update
  9.4 0.0 reduce-scatter.2.cloned.1.call-start
  9.5 0.8 copy.36
  10.3 0.1 eq.130
  10.5 0.1 eq.126
  10.6 0.6 reduce-window.6
  11.2 0.2 slice_reduce_fusion
  11.4 0.1 fusion.20
  11.5 0.1 reduce_sum.30
  11.7 0.1 copy.39
  12.6 1.8 %convolution_convert_fusion.2 = bf16[1024,2048]{1,0:T(8,128)(2,1)S(1)} fusion(bf16[128,2048]{1,0:T(8,128)(2,1)S(1)} %copy-done.8, bf16[128,2048]{1,0:T(8,128)(2,1)S(1)} %copy-done.9, f32[256]{0:T(256)S(1)} %bitcast.59, s32[256]{0:T(256)S(1)} %bitcast.57, f32[256]{0:T(256)S(1)} %bitcast.58, s32[256]{0:T(256)S(1)} %and_select_fusion, s32[256]{0:T(256)S(1)} %bitcast.56, ...), kind=kOutput, calls=%fused_computation.3 | convolution fusion | flops 1080295424 | bytes 5256192 | tf_op jit(solution)/shard_map/dot_general | solution.py:16
  14.4 57.3 %all_to_all.10 = bf16[16,64,2048]{2,1,0:T(8,128)(2,1)} all-to-all(bf16[16,64,2048]{2,1,0:T(8,128)(2,1)S(1)} %bitcast.51), channel_id=1, replica_groups=mesh['dp'=16,'expert'=16] {'expert'}, dimensions={0} | all-to-all | bytes 8388608 | tf_op jit(solution)/shard_map/all_to_all | solution.py:173
  71.8 3.8 %all-gather.2.cloned.1.call-done.w_ref = bf16[3,2048,768]{2,1,0:T(8,128)(2,1)} async-done(((bf16[3,128,768]{2,1,0:T(8,128)(2,1)}), bf16[3,2048,768]{2,1,0:T(8,128)(2,1)}) %all-gather.2.cloned.1.call-update) | async-done | bytes 9437200 | tf_op jit(solution)/shard_map/all_gather | solution.py:147
  75.6 13.4 %hidden.1 = (bf16[512,1536]{1,0:T(8,128)(2,1)}, bf16[512,768]{1,0:T(8,128)(2,1)}, f32[512,1]{1,0:T(8,128)}, bf16[512,1024]{1,0:T(8,128)(2,1)}, bf16[512,1024]{1,...) custom-call(s32[1]{0:T(128)} %bitcast.9.s_ref, bf16[16,2,32,2048]{3,2,1,0:T(8,128)(2,1)} %bitcast.48, ...), custom_call_target="tpu_custom_call" | custom-call | tf_op jit(solution)/shard_map/hidden/pallas_call | solution.py:74
  89.0 5.4 %convolution_convert_fusion = bf16[1024,1536]{1,0:T(8,128)(2,1)} fusion(bf16[512,1024]{1,0:T(8,128)(2,1)} %get-tuple-element.81, bf16[512,1536]{1,0:T(8,128)(2,1)} %get-tuple-element.98.grads_ref), kind=kOutput, calls=%fused_computation.1 | convolution fusion | flops 1612185600 | bytes 5767168 | tf_op jit(solution)/shard_map/dot_general | solution.py:20
  94.4 0.3 collective-permute-start
  94.6 2.2 %convolution_convert_fusion.5 = bf16[1024,768]{1,0:T(8,128)(2,1)} fusion(bf16[512,1024]{1,0:T(8,128)(2,1)S(1)} %copy-done.5, bf16[512,768]{1,0:T(8,128)(2,1)S(1)} %copy-done), kind=kOutput, calls=%fused_computation.7 | convolution fusion | flops 806092800 | bytes 3407872 | tf_op jit(solution)/shard_map/dot_general | solution.py:20
  96.8 0.3 collective-permute-start.2
  97.0 1.5 convolution_convert_fusion.6
  98.5 0.5 collective-permute-start.1
  99.1 3.6 %convolution_convert_fusion.1 = bf16[1024,1536]{1,0:T(8,128)(2,1)S(1)} fusion(bf16[512,1024]{1,0:T(8,128)(2,1)} %get-tuple-element.79, bf16[512,1536]{1,0:T(8,128)(2,1)} %get-tuple-element.98.grads_ref), kind=kOutput, calls=%fused_computation.2 | convolution fusion | flops 1612185600 | bytes 5767168 | tf_op jit(solution)/shard_map/dot_general | solution.py:20
  102.7 1.2 convolution_convert_fusion.7
  104.0 2.5 %add_convert_fusion = bf16[1024,1536]{1,0:T(8,128)(2,1)} fusion(bf16[1024,1536]{1,0:T(8,128)(2,1)S(1)} %collective-permute-done, bf16[1024,1536]{1,0:T(8,128)(2,1)S(1)} %convolution_convert_fusion.1), kind=kLoop, calls=%fused_computation | loop fusion | flops 6291456 | bytes 9437184 | tf_op jit(solution)/shard_map/convert_element_type | solution.py:188
  106.5 0.1 collective-permute-start.3
  106.6 3.6 %collective-permute-start.4 = (bf16[64,768]{1,0:T(8,128)(2,1)S(1)}, bf16[64,768]{1,0:T(8,128)(2,1)S(1)}, u32[]{:S(2)}, u32[]{:S(2)}) collective-permute-start(bf16[64,768]{1,0:T(8,128)(2,1)S(1)} %get-tuple-element.95), channel_id=1, source_target_pairs={{0,224},{16,240},{32,0},{48,16},{64,32},{80,48},{96,64},{112,80},{... | collective-permute-start | bytes 294920 | tf_op jit(solution)/shard_map/ppermute | solution.py:198
  110.2 1.0 convolution_convert_fusion.4
  111.2 10.2 %route_back.1 = bf16[512,2304]{1,0:T(8,128)(2,1)} custom-call(bf16[512,1536]{1,0:T(8,128)(2,1)} %get-tuple-element.98.grads_ref, bf16[3,2048,768]{2,1,0:T(8,128)(2,1)} %all-gather.2.cloned.1.call-done.w_ref, f32[512,1]{1,0:T(8,128)} %get-tuple-element.99.prob_ref), custom_call_target="tpu_custom_call" | custom-call | tf_op jit(solution)/shard_map/route_back/pallas_call | solution.py:116
  121.4 1.2 add_convert_fusion.13
  122.6 5.7 %all-to-all-start.1 = ((bf16[16,32,2304]{2,1,0:T(8,128)(2,1)}), bf16[16,32,2304]{2,1,0:T(8,128)(2,1)S(1)}, u32[]{:S(2)}, u32[]{:S(2)}) async-start(bf16[16,32,2304]{2,1,0:T(8,128)(2,1)} %bitcast.50), calls=%async_computation.1 | async-start | bytes 4718592 | tf_op jit(solution)/shard_map/all_to_all | solution.py:173
  128.3 0.1 collective-permute-start.5
  128.4 2.7 %collective-permute-start.6 = (bf16[128,768]{1,0:T(8,128)(2,1)S(1)}, bf16[128,768]{1,0:T(8,128)(2,1)S(1)}, u32[]{:S(2)}, u32[]{:S(2)}) collective-permute-start(bf16[128,768]{1,0:T(8,128)(2,1)S(1)} %get-tuple-element.111), channel_id=1, source_target_pairs={{0,224},{16,240},{32,0},{48,16},{64,32},{80,48},{96,64},{112,80},{... | collective-permute-start | bytes 589832 | tf_op jit(solution)/shard_map/ppermute | solution.py:198
  131.1 9.1 %collective-permute-done.5 = bf16[128,768]{1,0:T(8,128)(2,1)S(1)} collective-permute-done((bf16[128,768]{1,0:T(8,128)(2,1)S(1)}, bf16[128,768]{1,0:T(8,128)(2,1)S(1)}, u32[]{:S(2)}, u32[]{:S(2)}) %collective-permute-start.5) | collective-permute-done | bytes 196640 | tf_op jit(solution)/shard_map/ppermute | solution.py:198
  140.1 1.4 add_convert_fusion.7
  141.5 0.1 collective-permute-start.7
  141.6 2.7 %collective-permute-start.8 = (bf16[128,768]{1,0:T(8,128)(2,1)S(1)}, bf16[128,768]{1,0:T(8,128)(2,1)S(1)}, u32[]{:S(2)}, u32[]{:S(2)}) collective-permute-start(bf16[128,768]{1,0:T(8,128)(2,1)S(1)} %get-tuple-element.116), channel_id=1, source_target_pairs={{0,224},{16,240},{32,0},{48,16},{64,32},{80,48},{96,64},{112,80},{... | collective-permute-start | bytes 589832 | tf_op jit(solution)/shard_map/ppermute | solution.py:198
  144.3 8.9 %collective-permute-done.7 = bf16[128,768]{1,0:T(8,128)(2,1)S(1)} collective-permute-done((bf16[128,768]{1,0:T(8,128)(2,1)S(1)}, bf16[128,768]{1,0:T(8,128)(2,1)S(1)}, u32[]{:S(2)}, u32[]{:S(2)}) %collective-permute-start.7) | collective-permute-done | bytes 196640 | tf_op jit(solution)/shard_map/ppermute | solution.py:198
  153.2 1.4 add_convert_fusion.4
  154.6 2.8 %collective-permute-start.10 = (bf16[128,768]{1,0:T(8,128)(2,1)S(1)}, bf16[128,768]{1,0:T(8,128)(2,1)S(1)}, u32[]{:S(2)}, u32[]{:S(2)}) collective-permute-start(bf16[128,768]{1,0:T(8,128)(2,1)S(1)} %get-tuple-element.121), channel_id=1, source_target_pairs={{0,224},{16,240},{32,0},{48,16},{64,32},{80,48},{96,64},{112,80},{... | collective-permute-start | bytes 589832 | tf_op jit(solution)/shard_map/ppermute | solution.py:198
  157.4 2.6 %collective-permute-done.10 = bf16[128,768]{1,0:T(8,128)(2,1)S(1)} collective-permute-done((bf16[128,768]{1,0:T(8,128)(2,1)S(1)}, bf16[128,768]{1,0:T(8,128)(2,1)S(1)}, u32[]{:S(2)}, u32[]{:S(2)}) %collective-permute-start.10) | collective-permute-done | bytes 196640 | tf_op jit(solution)/shard_map/ppermute | solution.py:198
  160.0 3.4 %collective-permute-done.9 = bf16[128,768]{1,0:T(8,128)(2,1)S(1)} collective-permute-done((bf16[128,768]{1,0:T(8,128)(2,1)S(1)}, bf16[128,768]{1,0:T(8,128)(2,1)S(1)}, u32[]{:S(2)}, u32[]{:S(2)}) %collective-permute-start.9) | collective-permute-done | bytes 196640 | tf_op jit(solution)/shard_map/ppermute | solution.py:198
  163.5 1.1 add_convert_fusion.3
  164.6 0.1 convert_reduce_fusion
  164.7 0.2 select_reduce_fusion.1
  164.9 0.5 fusion.37
  165.4 1.3 convolution_convert_fusion.3
  166.7 1.8 %maximum_bitcast_fusion = bf16[1,128,2304]{2,1,0:T(8,128)(2,1)} fusion(bf16[128,768]{1,0:T(8,128)(2,1)S(1)} %add_convert_fusion.3, bf16[128,1536]{1,0:T(8,128)(2,1)} %reduce-scatter.2.cloned.1.call-done), kind=kLoop, calls=%fused_computation.17 | loop fusion | flops 1179648 | bytes 1179648 | tf_op jit(solution)/shard_map/broadcast_in_dim | solution.py:244
  (44 shorter events, 0.2 us)
Async XLA Ops:
  7.2 5.4 %copy-start.6 = (s32[128,2]{0,1:T(2,128)S(1)}, s32[128,2]{0,1:T(2,128)}, u32[]{:S(2)}) copy-start(s32[128,2]{0,1:T(2,128)} %param.10) | copy-start | bytes 3076
  7.2 5.4 %copy-start.7 = (bf16[128,2]{0,1:T(2,128)(2,1)S(1)}, bf16[128,2]{0,1:T(2,128)(2,1)}, u32[]{:S(2)}) copy-start(bf16[128,2]{0,1:T(2,128)(2,1)} %param.11) | copy-start | bytes 1540
  7.2 5.4 %copy-start.9 = (bf16[128,2048]{1,0:T(8,128)(2,1)S(1)}, bf16[128,2048]{1,0:T(8,128)(2,1)}, u32[]{:S(2)}) copy-start(bf16[128,2048]{1,0:T(8,128)(2,1)} %param.8) | copy-start | bytes 1572868
  7.2 5.4 %copy-start.8 = (bf16[128,2048]{1,0:T(8,128)(2,1)S(1)}, bf16[128,2048]{1,0:T(8,128)(2,1)}, u32[]{:S(2)}) copy-start(bf16[128,2048]{1,0:T(8,128)(2,1)} %param.9) | copy-start | bytes 1572868
  7.2 68.4 %all-gather.2.cloned.1.call-start = ((), (), s32[]{:S(2)}) async-start(), calls=%async_computation.3 | async-start | bytes 10027008 | tf_op jit(solution)/shard_map/all_gather | solution.py:147
  9.4 157.3 %reduce-scatter.2.cloned.1.call-start = ((), (), s32[]{:S(2)}) async-start(), calls=%async_computation.4 | async-start | bytes 3538944 | tf_op jit(solution)/shard_map/reduce_scatter | solution.py:217
  89.0 5.6 %copy-start = (bf16[512,768]{1,0:T(8,128)(2,1)S(1)}, bf16[512,768]{1,0:T(8,128)(2,1)}, u32[]{:S(2)}) copy-start(bf16[512,768]{1,0:T(8,128)(2,1)} %get-tuple-element.84) | copy-start | bytes 2359300
  89.0 5.6 %copy-start.5 = (bf16[512,1024]{1,0:T(8,128)(2,1)S(1)}, bf16[512,1024]{1,0:T(8,128)(2,1)}, u32[]{:S(2)}) copy-start(bf16[512,1024]{1,0:T(8,128)(2,1)} %get-tuple-element.85) | copy-start | bytes 3145732
  94.4 9.6 %collective-permute-start = (bf16[1024,1536]{1,0:T(8,128)(2,1)}, bf16[1024,1536]{1,0:T(8,128)(2,1)S(1)}, u32[]{:S(2)}, u32[]{:S(2)}) collective-permute-start(bf16[1024,1536]{1,0:T(8,128)(2,1)} %convolution_convert_fusion), channel_id=1, source_target_pairs={{0,16},{16,0},{32,48},{48,32},{64,80},{80,64},{96,112},{112,96},{1... | collective-permute-start | bytes 9437192 | tf_op jit(solution)/shard_map/ppermute | solution.py:191
  96.8 7.2 %collective-permute-start.2 = (bf16[1024,768]{1,0:T(8,128)(2,1)}, bf16[1024,768]{1,0:T(8,128)(2,1)}, u32[]{:S(2)}, u32[]{:S(2)}) collective-permute-start(bf16[1024,768]{1,0:T(8,128)(2,1)} %convolution_convert_fusion.5), channel_id=1, source_target_pairs={{0,16},{16,0},{32,48},{48,32},{64,80},{80,64},{96,112},{112,96},{1... | collective-permute-start | bytes 4718600 | tf_op jit(solution)/shard_map/ppermute | solution.py:191
  98.5 5.4 %collective-permute-start.1 = (bf16[128,768]{1,0:T(8,128)(2,1)S(1)}, bf16[128,768]{1,0:T(8,128)(2,1)S(1)}, u32[]{:S(2)}, u32[]{:S(2)}) collective-permute-start(bf16[128,768]{1,0:T(8,128)(2,1)S(1)} %convolution_convert_fusion.6), channel_id=1, source_target_pairs={{0,16},{16,0},{32,48},{48,32},{64,80},{80,64},{96,112},{112,96},{1... | collective-permute-start | bytes 589832 | tf_op jit(solution)/shard_map/ppermute | solution.py:191
  99.1 3.6 %copy-start.1 = (bf16[512,768]{1,0:T(8,128)(2,1)S(1)}, bf16[512,768]{1,0:T(8,128)(2,1)}, u32[]{:S(2)}) copy-start(bf16[512,768]{1,0:T(8,128)(2,1)} %get-tuple-element.84) | copy-start | bytes 2359300
  106.5 3.7 %copy-start.2 = (bf16[512,768]{1,0:T(8,128)(2,1)S(1)}, bf16[512,768]{1,0:T(8,128)(2,1)}, u32[]{:S(2)}) copy-start(bf16[512,768]{1,0:T(8,128)(2,1)} %get-tuple-element.84) | copy-start | bytes 2359300
  106.5 3.7 %copy-start.4 = (bf16[512,1024]{1,0:T(8,128)(2,1)S(1)}, bf16[512,1024]{1,0:T(8,128)(2,1)}, u32[]{:S(2)}) copy-start(bf16[512,1024]{1,0:T(8,128)(2,1)} %get-tuple-element.90) | copy-start | bytes 3145732
  106.5 14.9 %collective-permute-start.3 = (bf16[64,768]{1,0:T(8,128)(2,1)S(1)}, bf16[64,768]{1,0:T(8,128)(2,1)S(1)}, u32[]{:S(2)}, u32[]{:S(2)}) collective-permute-start(bf16[64,768]{1,0:T(8,128)(2,1)S(1)} %get-tuple-element.94), channel_id=1, source_target_pairs={{0,32},{16,48},{32,64},{48,80},{64,96},{80,112},{96,128},{112,144}... | collective-permute-start | bytes 294920 | tf_op jit(solution)/shard_map/ppermute | solution.py:198
  106.6 14.8 %collective-permute-start.4 = (bf16[64,768]{1,0:T(8,128)(2,1)S(1)}, bf16[64,768]{1,0:T(8,128)(2,1)S(1)}, u32[]{:S(2)}, u32[]{:S(2)}) collective-permute-start(bf16[64,768]{1,0:T(8,128)(2,1)S(1)} %get-tuple-element.95), channel_id=1, source_target_pairs={{0,224},{16,240},{32,0},{48,16},{64,32},{80,48},{96,64},{112,80},{... | collective-permute-start | bytes 294920 | tf_op jit(solution)/shard_map/ppermute | solution.py:198
  111.2 10.2 %copy-start.3 = (bf16[1024,768]{1,0:T(8,128)(2,1)}, bf16[1024,768]{1,0:T(8,128)(2,1)S(1)}, u32[]{:S(2)}) copy-start(bf16[1024,768]{1,0:T(8,128)(2,1)S(1)} %convolution_convert_fusion.4) | copy-start | bytes 4718596
  122.6 42.0 %all-to-all-start.1 = ((bf16[16,32,2304]{2,1,0:T(8,128)(2,1)}), bf16[16,32,2304]{2,1,0:T(8,128)(2,1)S(1)}, u32[]{:S(2)}, u32[]{:S(2)}) async-start(bf16[16,32,2304]{2,1,0:T(8,128)(2,1)} %bitcast.50), calls=%async_computation.1 | async-start | bytes 4718592 | tf_op jit(solution)/shard_map/all_to_all | solution.py:173
  128.3 11.8 %collective-permute-start.5 = (bf16[128,768]{1,0:T(8,128)(2,1)S(1)}, bf16[128,768]{1,0:T(8,128)(2,1)S(1)}, u32[]{:S(2)}, u32[]{:S(2)}) collective-permute-start(bf16[128,768]{1,0:T(8,128)(2,1)S(1)} %get-tuple-element.110), channel_id=1, source_target_pairs={{0,32},{16,48},{32,64},{48,80},{64,96},{80,112},{96,128},{112,144}... | collective-permute-start | bytes 589832 | tf_op jit(solution)/shard_map/ppermute | solution.py:198
  128.4 11.7 %collective-permute-start.6 = (bf16[128,768]{1,0:T(8,128)(2,1)S(1)}, bf16[128,768]{1,0:T(8,128)(2,1)S(1)}, u32[]{:S(2)}, u32[]{:S(2)}) collective-permute-start(bf16[128,768]{1,0:T(8,128)(2,1)S(1)} %get-tuple-element.111), channel_id=1, source_target_pairs={{0,224},{16,240},{32,0},{48,16},{64,32},{80,48},{96,64},{112,80},{... | collective-permute-start | bytes 589832 | tf_op jit(solution)/shard_map/ppermute | solution.py:198
  141.5 11.7 %collective-permute-start.7 = (bf16[128,768]{1,0:T(8,128)(2,1)S(1)}, bf16[128,768]{1,0:T(8,128)(2,1)S(1)}, u32[]{:S(2)}, u32[]{:S(2)}) collective-permute-start(bf16[128,768]{1,0:T(8,128)(2,1)S(1)} %get-tuple-element.115), channel_id=1, source_target_pairs={{0,32},{16,48},{32,64},{48,80},{64,96},{80,112},{96,128},{112,144}... | collective-permute-start | bytes 589832 | tf_op jit(solution)/shard_map/ppermute | solution.py:198
  141.6 11.6 %collective-permute-start.8 = (bf16[128,768]{1,0:T(8,128)(2,1)S(1)}, bf16[128,768]{1,0:T(8,128)(2,1)S(1)}, u32[]{:S(2)}, u32[]{:S(2)}) collective-permute-start(bf16[128,768]{1,0:T(8,128)(2,1)S(1)} %get-tuple-element.116), channel_id=1, source_target_pairs={{0,224},{16,240},{32,0},{48,16},{64,32},{80,48},{96,64},{112,80},{... | collective-permute-start | bytes 589832 | tf_op jit(solution)/shard_map/ppermute | solution.py:198
  154.6 5.5 %collective-permute-start.10 = (bf16[128,768]{1,0:T(8,128)(2,1)S(1)}, bf16[128,768]{1,0:T(8,128)(2,1)S(1)}, u32[]{:S(2)}, u32[]{:S(2)}) collective-permute-start(bf16[128,768]{1,0:T(8,128)(2,1)S(1)} %get-tuple-element.121), channel_id=1, source_target_pairs={{0,224},{16,240},{32,0},{48,16},{64,32},{80,48},{96,64},{112,80},{... | collective-permute-start | bytes 589832 | tf_op jit(solution)/shard_map/ppermute | solution.py:198
  157.4 6.0 %collective-permute-start.9 = (bf16[128,768]{1,0:T(8,128)(2,1)S(1)}, bf16[128,768]{1,0:T(8,128)(2,1)S(1)}, u32[]{:S(2)}, u32[]{:S(2)}) collective-permute-start(bf16[128,768]{1,0:T(8,128)(2,1)S(1)} %get-tuple-element.120), channel_id=1, source_target_pairs={{0,32},{16,48},{32,64},{48,80},{64,96},{80,112},{96,128},{112,144}... | collective-permute-start | bytes 589832 | tf_op jit(solution)/shard_map/ppermute | solution.py:198
Sparse Core Ops, SparseCore 0:
  10.5 65.0 all-gather.1
  106.6 51.3 reduce-scatter.1

commit v4 on v3

--- a/solution.py
+++ b/solution.py
@@ -34,7 +34,7 @@
     experts, _, capacity, width = received.shape
     slots, ff = experts * capacity, weights.shape[2]
 
-    def body(s_ref, rows_ref, scaled_ref, w_ref, grads_ref, act_ref, prob_ref, *apart):
+    def body(s_ref, rows_ref, scaled_ref, w_ref, gate_ref, up_ref, act_ref, prob_ref, *apart):
         rows = rows_ref[...].reshape(slots, width)
         scaled = scaled_ref[...].reshape(slots, width)
         gate = dot(rows, w_ref[0])
@@ -43,15 +43,8 @@
         sig = jax.nn.sigmoid(gate)
         silu = gate * sig
         act = (silu * up).astype(BF16)
-        d_gate = (back * up * (sig * (1.0 + gate * (1.0 - sig)))).astype(BF16)
-        d_up = (back * silu).astype(BF16)
-        for j in range(ff // BLOCK):
-
-            @pl.when(pl.program_id(0) == j)
-            def _():
-                grads_ref[:, j * BLOCK : (j + 1) * BLOCK] = d_gate
-                grads_ref[:, ff + j * BLOCK : ff + (j + 1) * BLOCK] = d_up
-
+        gate_ref[...] = (back * up * (sig * (1.0 + gate * (1.0 - sig)))).astype(BF16)
+        up_ref[...] = (back * silu).astype(BF16)
         act_ref[...] = act
         part = jnp.sum(act.astype(F32) * back, axis=1, keepdims=True)
 
@@ -82,14 +75,16 @@
                 pl.BlockSpec((3, width, BLOCK), lambda j, s: (0, 0, j)),
             ],
             out_specs=[
-                pl.BlockSpec((slots, 2 * ff), lambda j, s: (0, 0)),
+                pl.BlockSpec((slots, BLOCK), lambda j, s: (0, j)),
+                pl.BlockSpec((slots, BLOCK), lambda j, s: (0, j)),
                 pl.BlockSpec((slots, BLOCK), lambda j, s: (0, j)),
                 pl.BlockSpec((slots, 1), lambda j, s: (0, 0)),
             ]
             + [pl.BlockSpec((slots, width // 2), lambda j, s: (0, 0))] * 4,
         ),
         out_shape=[
-            jax.ShapeDtypeStruct((slots, 2 * ff), BF16),
+            jax.ShapeDtypeStruct((slots, ff), BF16),
+            jax.ShapeDtypeStruct((slots, ff), BF16),
             jax.ShapeDtypeStruct((slots, ff), BF16),
             jax.ShapeDtypeStruct((slots, 1), F32),
         ]
@@ -99,14 +94,14 @@
     )(core[None].astype(jnp.int32), received, received, weights)
 
 
-def route_back(grads, weights, prob):
-    slots, width, ff = grads.shape[0], *weights.shape[1:]
+def route_back(d_gate, d_up, weights, prob):
+    slots, width, ff = d_gate.shape[0], *weights.shape[1:]
     steps = width // BLOCK
 
-    def body(grads_ref, w_ref, prob_ref, out_ref):
+    def body(gate_ref, up_ref, w_ref, prob_ref, out_ref):
         @pl.when(pl.program_id(0) < steps)
         def _():
-            value = dot_last(grads_ref[:, :ff], w_ref[0]) + dot_last(grads_ref[:, ff:], w_ref[1])
+            value = dot_last(gate_ref[...], w_ref[0]) + dot_last(up_ref[...], w_ref[1])
             out_ref[...] = value.astype(BF16)
 
         @pl.when(pl.program_id(0) == steps)
@@ -117,7 +112,8 @@
         body,
         grid=(steps + 1,),
         in_specs=[
-            pl.BlockSpec((slots, 2 * ff), lambda i: (0, 0)),
+            pl.BlockSpec((slots, ff), lambda i: (0, 0)),
+            pl.BlockSpec((slots, ff), lambda i: (0, 0)),
             pl.BlockSpec((2, BLOCK, ff), lambda i: (0, jnp.minimum(i, steps - 1), 0)),
             pl.BlockSpec((slots, 1), lambda i: (0, 0)),
         ],
@@ -125,7 +121,7 @@
         out_shape=jax.ShapeDtypeStruct((slots, width + BLOCK), BF16),
         compiler_params=params(),
         name="route_back",
-    )(grads, weights, prob)
+    )(d_gate, d_up, weights, prob)
 
 
 def per_device(
@@ -139,10 +135,8 @@
     slots = experts * capacity
     ff = gate_weight.shape[2]
     dp = lax.axis_index("dp")
-    chip, core = dp // 2, dp % 2
+    core = dp % 2
     swap = [(2 * z + c, 2 * z + 1 - c) for z in range(chips) for c in range(2)]
-    up_ring = [(2 * z + c, 2 * ((z + 1) % chips) + c) for z in range(chips) for c in range(2)]
-    down_ring = [(2 * z + c, 2 * ((z - 1) % chips) + c) for z in range(chips) for c in range(2)]
 
     weights = lax.all_gather(
         jnp.concatenate((gate_weight, up_weight, down_weight), axis=0), "dp", axis=1, tiled=True
@@ -174,13 +168,11 @@
             value.reshape(experts, lines, -1), "expert", split_axis=0, concat_axis=0, tiled=True
         )
 
-    far = chips // 2
-    at = [(chip + n) % chips for n in range(chips)]
-    send, at, core, target = lax.optimization_barrier((send, at, core, target))
-    received, at, core, target = lax.optimization_barrier(
-        (exchange(send, 2 * capacity), at, core, target)
-    )
-    grads, act, prob_part, rows_own, rows_other, scaled_own, scaled_other = hidden(
+    send, core, target = lax.optimization_barrier((send, core, target))
+    received, core, target = lax.optimization_barrier(
+        (exchange(send, 2 * capacity), core, target)
+    )
+    d_gate, d_up, act, prob_part, rows_own, rows_other, scaled_own, scaled_other = hidden(
         received.reshape(experts, 2, capacity, width), weights, core
     )
 
@@ -193,55 +185,27 @@
     def grad_of(left, right):
         return dot_rows(left, right).astype(BF16)
 
-    def both_ways(right, left):
-        right, left = lax.optimization_barrier((right, left))
-        right, left = lax.ppermute(right, "dp", up_ring), lax.ppermute(left, "dp", down_ring)
-        return lax.optimization_barrier((right, left))
-
-    gate_up_other = swapped(grad_of(rows_other, grads))
-    far_own, far_other = (
-        grad_of(lax.dynamic_slice(lines, (0, at[far] * LANES), (slots, LANES)), act)
-        for lines in (scaled_own, scaled_other)
-    )
-    far_other = swapped(far_other)
-    other = swapped(grad_of(scaled_other, act))
-    gate_up_own = grad_of(rows_own, grads)
-    gate_up_own, gate_up_other, far_own, far_other, other = lax.optimization_barrier(
-        (gate_up_own, gate_up_other, far_own, far_other, other)
-    )
-    gate_up_pair = add(gate_up_own, gate_up_other)
-    far_sum = add(far_own, far_other)
-    gate_up_pair, far_sum, scaled_own, grads = lax.optimization_barrier(
-        (gate_up_pair, far_sum, scaled_own, grads)
-    )
-    gate_up_sum = lax.psum_scatter(
-        gate_up_pair,
+    other = []
+    for lines, grad in ((scaled_other, act), (rows_other, d_gate), (rows_other, d_up)):
+        if other:
+            lines, grad, other[-1] = lax.optimization_barrier((lines, grad, other[-1]))
+        other.append(grad_of(lines, grad))
+    other = [swapped(part) for part in other]
+    own_other = other
+    own = [
+        grad_of(lines, grad) for lines, grad in ((scaled_own, act), (rows_own, d_gate), (rows_own, d_up))
+    ]
+    pairs = jnp.zeros((chips * LANES, 3 * ff), BF16)
+    for n, mine, theirs in zip((2, 0, 1), own, own_other, strict=True):
+        pairs = lax.dynamic_update_slice(pairs, add(mine, theirs), (0, n * ff))
+    weight_grad = lax.psum_scatter(
+        pairs,
         "dp",
         scatter_dimension=0,
         axis_index_groups=[[2 * z + c for z in range(chips)] for c in range(2)],
         tiled=True,
-    )
-    right, left = both_ways(far_sum[: LANES // 2], far_sum[LANES // 2 :])
-    own = grad_of(scaled_own, act)
-    back = route_back(grads, weights, prob_part)
-    right, left, back = lax.optimization_barrier((right, left, back))
-
-    def pair(n):
-        where, size = (at[n] * LANES, 0), (LANES, ff)
-        return add(lax.dynamic_slice(own, where, size), lax.dynamic_slice(other, where, size))
-
-    zeros = jnp.zeros((LANES // 2, ff), BF16)
-    right = jnp.concatenate((right, zeros), axis=0)
-    left = jnp.concatenate((zeros, left), axis=0)
-    for n in range(far - 1, 0, -1):
-        right, left = add(pair(n), right), add(pair(chips - n), left)
-        if n == far - 1:
-            right, left, back = lax.optimization_barrier((right, left, back))
-            back = exchange(back, capacity)
-        right, left = both_ways(right, left)
-    down_sum = add(pair(0), right, left)
-    down_sum, gate_up_sum = lax.optimization_barrier((down_sum, gate_up_sum))
-    weight_grad = jnp.concatenate((gate_up_sum, down_sum), axis=1)[None]
+    )[None]
+    back = exchange(route_back(d_gate, d_up, weights, prob_part), capacity)
 
     back = back.reshape(slots, width + BLOCK)
     slot = jnp.arange(slots, dtype=jnp.int32)[:, None]

time: 178 us -> 169 us (0.949); the launches traced: 175 us -> 169 us
  waiting for transfers between devices: 27.9 us -> 42.6 us
  starting transfers between devices: 18.9 us -> 8.07 us
  other arithmetic: 13 us -> 4.89 us
  matrix products: 18 us -> 14.6 us
  local copies, waits for them, and re-layouts: 1.52 us -> 4.05 us
    all_to_all x1, waiting for transfers between devices: 0.01 us -> 36.4 us  [exchange(): lax.all_to_all(value.reshape(experts, lines, -1), 'expert', split_axis=0,...]
    ppermute x8 -> x0, waiting for transfers between devices: 24 us -> none  [the longest x4 21.4 us: both_ways(): lax.ppermute(right, 'dp', up_ring)]
    ppermute x8 -> x0, starting transfers between devices: 12 us -> none  [the longest x4 11.8 us: both_ways(): lax.ppermute(left, 'dp', down_ring)]
    convert_element_type x6 -> x0, other arithmetic: 7.55 us -> none  [add(): return sum((value.astype(F32) for value in values)).astype(BF16)]
    reduce_scatter x1, waiting for transfers between devices: 0.01 us -> 4.56 us  [per_device(): lax.psum_scatter(pairs, 'dp', scatter_dimension=0, axis_index_groups=[[2...]
    dot_general x7, matrix products: 16.1 us -> 11.6 us  [dot_rows(): lax.dot_general(left, right, (((0,), (0,)), ((), ())), preferred_element_...]
    dynamic_update_slice x0 -> x1, local copies, waits for them, and re-layouts: none -> 2.56 us  [per_device(): pairs = lax.dynamic_update_slice(pairs, add(mine, theirs), (0, n * ff))]
    all_gather x1, waiting for transfers between devices: 3.82 us -> 1.61 us  [per_device(): lax.all_gather(jnp.concatenate((gate_weight, up_weight, down_weight), axi...]
  transfers between devices with their start and end apart: 14 -> 6, of which waited for: 5 -> 4; matrix products, arithmetic and copies ran while one was open for 12% -> 10% of each run, Pallas kernels for 6% -> 6%
where the time goes in v4:
time: 169 us
  blocking collectives  57.3 us (34%)
  waiting for transfers between devices  42.6 us (25%)
  Pallas kernels  22.4 us (13%)
  between operations  14.9 us (9%)
  matrix products  14.6 us (9%)
  starting transfers between devices  8.07 us (5%)
  other arithmetic  4.89 us (3%)
  local copies, waits for them, and re-layouts  4.05 us (2%)
    all_to_all x1, blocking collectives, exchange(): lax.all_to_all(value.reshape(experts, lines, -1), 'expert', split_axis=0,...  57.3 us
    all_to_all x1, waiting for transfers between devices, exchange(): lax.all_to_all(value.reshape(experts, lines, -1), 'expert', split_axis=0,...  36.4 us
    pallas_call x1, Pallas kernels, hidden(): pl.pallas_call(body, grid_spec=pltpu.PrefetchScalarGridSpec(num_scalar_pr...  12.8 us
    dot_general x7, matrix products, dot_rows(): lax.dot_general(left, right, (((0,), (0,)), ((), ())), preferred_element_...  11.6 us
    pallas_call x1, Pallas kernels, route_back(): pl.pallas_call(body, grid=(steps + 1,), in_specs=[pl.BlockSpec((slots, ff...  9.57 us
    all_to_all x1, starting transfers between devices, exchange(): lax.all_to_all(value.reshape(experts, lines, -1), 'expert', split_axis=0,...  6.65 us
    reduce_scatter x1, waiting for transfers between devices, per_device(): lax.psum_scatter(pairs, 'dp', scatter_dimension=0, axis_index_groups=[[2...  4.56 us
  transfers between devices with their start and end apart: 6, of which 4 were waited for; matrix products, arithmetic and copies ran while one was open for 10% of the time, Pallas kernels for 6%

profile of v4, /device:TPU:1, one launch (start us, length us, event | category | flops | bytes accessed | tf_op | source)
XLA Modules:
  0.0 168.8 jit_solution(17712520996226027509)
XLA Ops:
  7.2 0.0 all-gather.2.cloned.1.call-start
  7.2 2.0 %pad_maximum_fusion = bf16[3,128,768]{2,1,0:T(8,128)(2,1)} fusion(bf16[1,128,768]{2,1,0:T(8,128)(2,1)} %param.15, bf16[1,128,768]{2,1,0:T(8,128)(2,1)} %param.14, bf16[1,128,768]{2,1,0:T(8,128)(2,1)} %param.13), kind=kLoop, calls=%fused_computation.20 | loop fusion | flops 589824 | bytes 1179648 | tf_op jit(solution)/shard_map/concatenate | solution.py:142
  9.2 0.0 all-gather.2.cloned.1.call-update
  9.2 0.0 reduce-scatter.2.cloned.1.call-start
  9.3 0.8 copy.36
  10.1 0.1 eq.122
  10.2 0.1 eq.118
  11.0 0.6 reduce-window.6
  11.6 0.2 slice_reduce_fusion
  11.8 0.1 fusion.20
  11.9 0.1 reduce_sum.30
  12.1 0.1 copy.39
  12.2 0.7 convert_select_fusion
  12.9 0.7 multiply_add_fusion
  13.5 3.0 %convolution_convert_fusion = bf16[1024,2048]{1,0:T(8,128)(2,1)S(1)} fusion(bf16[128,2048]{1,0:T(8,128)(2,1)} %param.9, bf16[128,2048]{1,0:T(8,128)(2,1)} %param.8, f32[256]{0:T(256)S(1)} %bitcast.58, s32[256]{0:T(256)S(1)} %bitcast.60, f32[256]{0:T(256)S(1)} %bitcast.57, s32[256]{0:T(256)S(1)} %and_select_fusion, s32[256]{0:T(256)S(1)} %bitcast.59, ...), kind=kOutput, calls=%fused_computation | convolution fusion | flops 1080295424 | bytes 5256192 | tf_op jit(solution)/shard_map/dot_general | solution.py:16
  16.6 57.3 %all_to_all.10 = bf16[16,64,2048]{2,1,0:T(8,128)(2,1)} all-to-all(bf16[16,64,2048]{2,1,0:T(8,128)(2,1)S(1)} %bitcast.52), channel_id=1, replica_groups=mesh['dp'=16,'expert'=16] {'expert'}, dimensions={0} | all-to-all | bytes 8388608 | tf_op jit(solution)/shard_map/all_to_all | solution.py:167
  73.9 1.6 all-gather.2.cloned.1.call-done.w_ref
  75.5 12.8 %hidden.1 = (bf16[512,768]{1,0:T(8,128)(2,1)}, bf16[512,768]{1,0:T(8,128)(2,1)}, bf16[512,768]{1,0:T(8,128)(2,1)}, f32[512,1]{1,0:T(8,128)}, bf16[512,1024]{1,0:...) custom-call(s32[1]{0:T(128)} %bitcast.9.s_ref, ...), custom_call_target="tpu_custom_call" | custom-call | tf_op jit(solution)/shard_map/hidden/pallas_call | solution.py:67
  88.3 0.0 copy-start
  88.4 0.0 copy-start.5
  88.4 2.6 %convolution_convert_fusion.6 = bf16[1024,768]{1,0:T(8,128)(2,1)S(1)} fusion(bf16[512,1024]{1,0:T(8,128)(2,1)} %get-tuple-element.35, bf16[512,768]{1,0:T(8,128)(2,1)} %get-tuple-element.33), kind=kOutput, calls=%fused_computation.10 | convolution fusion | flops 806092800 | bytes 3407872 | tf_op jit(solution)/shard_map/dot_general | solution.py:20
  91.0 0.0 copy-start.1
  91.0 0.5 collective-permute-start
  91.5 0.0 copy-done
  91.5 0.0 copy-done.5
  91.5 1.0 convolution_convert_fusion.4
  92.5 0.0 copy-start.4
  92.5 0.0 copy-start.6
  92.5 0.2 collective-permute-start.1
  92.7 1.0 convolution_convert_fusion.2
  93.8 0.7 collective-permute-start.2
  94.4 0.1 collective-permute-done
  94.5 0.0 copy-done.6
  94.5 1.1 add_convert_fusion.2
  95.6 2.6 %dynamic_update_slice.9 = bf16[1024,2304]{1,0:T(8,128)(2,1)} pad(bf16[1024,768]{1,0:T(8,128)(2,1)S(1)} %add_convert_fusion.2, bf16[]{:T(256)} %constant.97.clone.1), padding=0_0x1536_0 | pad | bytes 6291458 | tf_op jit(solution)/shard_map/dynamic_update_slice | solution.py:200
  98.2 0.0 collective-permute-done.1
  98.2 2.3 %fusion.1 = bf16[1024,2304]{1,0:T(8,128)(2,1)} fusion(bf16[1024,2304]{1,0:T(8,128)(2,1)} %dynamic_update_slice.9, bf16[1024,768]{1,0:T(8,128)(2,1)S(1)} %collective-permute-done.1, bf16[512,1024]{1,0:T(8,128)(2,1)S(1)} %copy-done.3, bf16[512,768]{1,0:T(8,128)(2,1)S(1)} %copy-done), kind=kOutput, calls=%fused_computation.12 | convolution fusion | flops 809238528 | bytes 4980736 | tf_op jit(solution)/shard_map/dot_general | solution.py:20
  100.4 0.0 collective-permute-done.2
  100.4 2.3 %fusion.2 = bf16[1024,2304]{1,0:T(8,128)(2,1)} fusion(bf16[1024,2304]{1,0:T(8,128)(2,1)} %fusion.1, bf16[1024,768]{1,0:T(8,128)(2,1)S(1)} %collective-permute-done.2, bf16[512,1024]{1,0:T(8,128)(2,1)S(1)} %copy-done.3, bf16[512,768]{1,0:T(8,128)(2,1)S(1)} %copy-done.1), kind=kOutput, calls=%fused_computation.13 | convolution fusion | flops 809238528 | bytes 4980736 | tf_op jit(solution)/shard_map/dot_general | solution.py:20
  102.7 0.0 reduce-scatter.2.cloned.1.call-update
  102.8 9.6 %route_back.1 = bf16[512,2304]{1,0:T(8,128)(2,1)} custom-call(bf16[512,768]{1,0:T(8,128)(2,1)} %get-tuple-element.39.gate_ref, bf16[512,768]{1,0:T(8,128)(2,1)} %get-tuple-element.42.up_ref, bf16[3,2048,768]{2,1,0:T(8,128)(2,1)} %all-gather.2.cloned.1.call-done.w_ref, f32[512,1]{1,0:T(8,128)} %get-tuple-element.31.prob_ref), custom_call_target="tpu_custom_call" | custom-call | tf_op jit(solution)/shard_map/route_back/pallas_call | solution.py:111
  112.3 6.6 %all-to-all-start.1 = ((bf16[16,32,2304]{2,1,0:T(8,128)(2,1)}), bf16[16,32,2304]{2,1,0:T(8,128)(2,1)S(1)}, u32[]{:S(2)}, u32[]{:S(2)}) async-start(bf16[16,32,2304]{2,1,0:T(8,128)(2,1)} %bitcast.51), calls=%async_computation.1 | async-start | bytes 4718592 | tf_op jit(solution)/shard_map/all_to_all | solution.py:167
  119.0 36.4 %all-to-all-done.1 = bf16[16,32,2304]{2,1,0:T(8,128)(2,1)S(1)} async-done(((bf16[16,32,2304]{2,1,0:T(8,128)(2,1)}), bf16[16,32,2304]{2,1,0:T(8,128)(2,1)S(1)}, u32[]{:S(2)}, u32[]{:S(2)}) %all-to-all-start.1) | async-done | bytes 2359328 | tf_op jit(solution)/shard_map/all_to_all | solution.py:167
  155.4 0.1 convert_reduce_fusion
  155.5 0.2 select_reduce_fusion.1
  155.6 0.5 fusion.35
  156.2 1.3 convolution_convert_fusion.1
  157.4 4.6 %reduce-scatter.2.cloned.1.call-done = bf16[128,2304]{1,0:T(8,128)(2,1)} async-done(((bf16[1024,2304]{1,0:T(8,128)(2,1)}), bf16[128,2304]{1,0:T(8,128)(2,1)}) %reduce-scatter.2.cloned.1.call-update) | async-done | bytes 589840 | tf_op jit(solution)/shard_map/reduce_scatter | solution.py:201
  (15 shorter events, 0.1 us)
Async XLA Ops:
  7.2 68.4 %all-gather.2.cloned.1.call-start = ((), (), s32[]{:S(2)}) async-start(), calls=%async_computation.3 | async-start | bytes 10027008 | tf_op jit(solution)/shard_map/all_gather | solution.py:141
  9.2 152.8 %reduce-scatter.2.cloned.1.call-start = ((), (), s32[]{:S(2)}) async-start(), calls=%async_computation.4 | async-start | bytes 5308416 | tf_op jit(solution)/shard_map/reduce_scatter | solution.py:201
  88.3 3.1 %copy-start = (bf16[512,768]{1,0:T(8,128)(2,1)S(1)}, bf16[512,768]{1,0:T(8,128)(2,1)}, u32[]{:S(2)}) copy-start(bf16[512,768]{1,0:T(8,128)(2,1)} %get-tuple-element.39.gate_ref) | copy-start | bytes 2359300
  88.4 3.1 %copy-start.5 = (bf16[512,1024]{1,0:T(8,128)(2,1)S(1)}, bf16[512,1024]{1,0:T(8,128)(2,1)}, u32[]{:S(2)}) copy-start(bf16[512,1024]{1,0:T(8,128)(2,1)} %get-tuple-element.41) | copy-start | bytes 3145732
  91.0 1.8 %copy-start.1 = (bf16[512,768]{1,0:T(8,128)(2,1)S(1)}, bf16[512,768]{1,0:T(8,128)(2,1)}, u32[]{:S(2)}) copy-start(bf16[512,768]{1,0:T(8,128)(2,1)} %get-tuple-element.42.up_ref) | copy-start | bytes 2359300
  91.0 3.5 %collective-permute-start = (bf16[1024,768]{1,0:T(8,128)(2,1)S(1)}, bf16[1024,768]{1,0:T(8,128)(2,1)S(1)}, u32[]{:S(2)}, u32[]{:S(2)}) collective-permute-start(bf16[1024,768]{1,0:T(8,128)(2,1)S(1)} %convolution_convert_fusion.6), channel_id=1, source_target_pairs={{0,16},{16,0},{32,48},{48,32},{64,80},{80,64},{96,112},{112,96},{1... | collective-permute-start | bytes 4718600 | tf_op jit(solution)/shard_map/ppermute | solution.py:183
  92.5 2.0 %copy-start.4 = (bf16[512,1024]{1,0:T(8,128)(2,1)S(1)}, bf16[512,1024]{1,0:T(8,128)(2,1)}, u32[]{:S(2)}) copy-start(bf16[512,1024]{1,0:T(8,128)(2,1)} %get-tuple-element.32) | copy-start | bytes 3145732
  92.5 2.0 %copy-start.6 = (bf16[512,768]{1,0:T(8,128)(2,1)S(1)}, bf16[512,768]{1,0:T(8,128)(2,1)}, u32[]{:S(2)}) copy-start(bf16[512,768]{1,0:T(8,128)(2,1)} %get-tuple-element.33) | copy-start | bytes 2359300
  92.5 5.6 %collective-permute-start.1 = (bf16[1024,768]{1,0:T(8,128)(2,1)S(1)}, bf16[1024,768]{1,0:T(8,128)(2,1)S(1)}, u32[]{:S(2)}, u32[]{:S(2)}) collective-permute-start(bf16[1024,768]{1,0:T(8,128)(2,1)S(1)} %convolution_convert_fusion.4), channel_id=1, source_target_pairs={{0,16},{16,0},{32,48},{48,32},{64,80},{80,64},{96,112},{112,96},{1... | collective-permute-start | bytes 4718600 | tf_op jit(solution)/shard_map/ppermute | solution.py:183
  93.8 6.7 %collective-permute-start.2 = (bf16[1024,768]{1,0:T(8,128)(2,1)S(1)}, bf16[1024,768]{1,0:T(8,128)(2,1)S(1)}, u32[]{:S(2)}, u32[]{:S(2)}) collective-permute-start(bf16[1024,768]{1,0:T(8,128)(2,1)S(1)} %convolution_convert_fusion.2), channel_id=1, source_target_pairs={{0,16},{16,0},{32,48},{48,32},{64,80},{80,64},{96,112},{112,96},{1... | collective-permute-start | bytes 4718600 | tf_op jit(solution)/shard_map/ppermute | solution.py:183
  95.6 2.6 %copy-start.3 = (bf16[512,1024]{1,0:T(8,128)(2,1)S(1)}, bf16[512,1024]{1,0:T(8,128)(2,1)}, u32[]{:S(2)}) copy-start(bf16[512,1024]{1,0:T(8,128)(2,1)} %get-tuple-element.37) | copy-start | bytes 3145732
  112.3 43.3 %copy-start.2 = (bf16[128,2]{0,1:T(2,128)(2,1)S(1)}, bf16[128,2]{0,1:T(2,128)(2,1)}, u32[]{:S(2)}) copy-start(bf16[128,2]{0,1:T(2,128)(2,1)} %param.11) | copy-start | bytes 1540
  112.3 43.0 %all-to-all-start.1 = ((bf16[16,32,2304]{2,1,0:T(8,128)(2,1)}), bf16[16,32,2304]{2,1,0:T(8,128)(2,1)S(1)}, u32[]{:S(2)}, u32[]{:S(2)}) async-start(bf16[16,32,2304]{2,1,0:T(8,128)(2,1)} %bitcast.51), calls=%async_computation.1 | async-start | bytes 4718592 | tf_op jit(solution)/shard_map/all_to_all | solution.py:167
Sparse Core Ops, SparseCore 0:
  10.4 65.0 all-gather.1
  102.9 59.0 reduce-scatter.1

commit v5 on v4

--- a/solution.py
+++ b/solution.py
@@ -43,9 +43,17 @@
         sig = jax.nn.sigmoid(gate)
         silu = gate * sig
         act = (silu * up).astype(BF16)
-        gate_ref[...] = (back * up * (sig * (1.0 + gate * (1.0 - sig)))).astype(BF16)
-        up_ref[...] = (back * silu).astype(BF16)
-        act_ref[...] = act
+        d_gate = (back * up * (sig * (1.0 + gate * (1.0 - sig)))).astype(BF16)
+        d_up = (back * silu).astype(BF16)
+        for j in range(ff // BLOCK):
+
+            @pl.when(pl.program_id(0) == j)
+            def _():
+                at = slice(j * BLOCK, (j + 1) * BLOCK)
+                gate_ref[:, at] = d_gate
+                up_ref[:, at] = d_up
+                act_ref[:, at] = act
+
         part = jnp.sum(act.astype(F32) * back, axis=1, keepdims=True)
 
         @pl.when(pl.program_id(0) == 0)
@@ -74,21 +82,13 @@
                 pl.BlockSpec((experts, 1, capacity, width), lambda j, s: (0, 1, 0, 0)),
                 pl.BlockSpec((3, width, BLOCK), lambda j, s: (0, 0, j)),
             ],
-            out_specs=[
-                pl.BlockSpec((slots, BLOCK), lambda j, s: (0, j)),
-                pl.BlockSpec((slots, BLOCK), lambda j, s: (0, j)),
-                pl.BlockSpec((slots, BLOCK), lambda j, s: (0, j)),
-                pl.BlockSpec((slots, 1), lambda j, s: (0, 0)),
-            ]
-            + [pl.BlockSpec((slots, width // 2), lambda j, s: (0, 0))] * 4,
+            out_specs=[pl.BlockSpec(memory_space=pltpu.VMEM)] * 3
+            + [pl.BlockSpec((slots, 1), lambda j, s: (0, 0))]
+            + [pl.BlockSpec(memory_space=pltpu.VMEM)] * 4,
         ),
-        out_shape=[
-            jax.ShapeDtypeStruct((slots, ff), BF16),
-            jax.ShapeDtypeStruct((slots, ff), BF16),
-            jax.ShapeDtypeStruct((slots, ff), BF16),
-            jax.ShapeDtypeStruct((slots, 1), F32),
-        ]
-        + [jax.ShapeDtypeStruct((slots, width // 2), BF16)] * 4,
+        out_shape=[pltpu.VMEM((slots, ff), BF16)] * 3
+        + [jax.ShapeDtypeStruct((slots, 1), F32)]
+        + [pltpu.VMEM((slots, width // 2), BF16)] * 4,
         compiler_params=params(),
         name="hidden",
     )(core[None].astype(jnp.int32), received, received, weights)

time: 169 us -> 166 us (0.982)
  no operation moved by 1% of the time
where the time goes in v5:
time: 166 us
  blocking collectives  57.3 us (35%)
  waiting for transfers between devices  42.7 us (26%)
  Pallas kernels  21 us (13%)
  between operations  14.8 us (9%)
  matrix products  13 us (8%)
  starting transfers between devices  8.07 us (5%)
  other arithmetic  4.89 us (3%)
  local copies, waits for them, and re-layouts  4.02 us (2%)
    all_to_all x1, blocking collectives, exchange(): lax.all_to_all(value.reshape(experts, lines, -1), 'expert', split_axis=0,...  57.3 us
    all_to_all x1, waiting for transfers between devices, exchange(): lax.all_to_all(value.reshape(experts, lines, -1), 'expert', split_axis=0,...  36.3 us
    pallas_call x1, Pallas kernels, hidden(): pl.pallas_call(body, grid_spec=pltpu.PrefetchScalarGridSpec(num_scalar_pr...  11.4 us
    dot_general x7, matrix products, dot_rows(): lax.dot_general(left, right, (((0,), (0,)), ((), ())), preferred_element_...  9.95 us
    pallas_call x1, Pallas kernels, route_back(): pl.pallas_call(body, grid=(steps + 1,), in_specs=[pl.BlockSpec((slots, ff...  9.56 us
    all_to_all x1, starting transfers between devices, exchange(): lax.all_to_all(value.reshape(experts, lines, -1), 'expert', split_axis=0,...  6.66 us
    reduce_scatter x1, waiting for transfers between devices, per_device(): lax.psum_scatter(pairs, 'dp', scatter_dimension=0, axis_index_groups=[[2...  4.57 us
  transfers between devices with their start and end apart: 6, of which 4 were waited for; matrix products, arithmetic and copies ran while one was open for 10% of the time, Pallas kernels for 6%

profile of v5, /device:TPU:1, one launch (start us, length us, event | category | flops | bytes accessed | tf_op | source)
XLA Modules:
  0.0 165.8 jit_solution(13109274392998705886)
XLA Ops:
  7.2 0.0 all-gather.2.cloned.1.call-start
  7.2 2.0 %pad_maximum_fusion = bf16[3,128,768]{2,1,0:T(8,128)(2,1)} fusion(bf16[1,128,768]{2,1,0:T(8,128)(2,1)} %param.15, bf16[1,128,768]{2,1,0:T(8,128)(2,1)} %param.14, bf16[1,128,768]{2,1,0:T(8,128)(2,1)} %param.13), kind=kLoop, calls=%fused_computation.20 | loop fusion | flops 589824 | bytes 1179648 | tf_op jit(solution)/shard_map/concatenate | solution.py:142
  9.2 0.0 all-gather.2.cloned.1.call-update
  9.2 0.0 reduce-scatter.2.cloned.1.call-start
  9.3 0.8 copy.36
  10.1 0.1 eq.122
  10.2 0.1 eq.118
  11.0 0.6 reduce-window.6
  11.6 0.2 slice_reduce_fusion
  11.8 0.1 fusion.20
  11.9 0.1 reduce_sum.30
  12.1 0.1 copy.39
  12.2 0.7 convert_select_fusion
  12.9 0.7 multiply_add_fusion
  13.5 3.0 %convolution_convert_fusion = bf16[1024,2048]{1,0:T(8,128)(2,1)S(1)} fusion(bf16[128,2048]{1,0:T(8,128)(2,1)} %param.9, bf16[128,2048]{1,0:T(8,128)(2,1)} %param.8, f32[256]{0:T(256)S(1)} %bitcast.58, s32[256]{0:T(256)S(1)} %bitcast.60, f32[256]{0:T(256)S(1)} %bitcast.57, s32[256]{0:T(256)S(1)} %and_select_fusion, s32[256]{0:T(256)S(1)} %bitcast.59, ...), kind=kOutput, calls=%fused_computation | convolution fusion | flops 1080295424 | bytes 5256192 | tf_op jit(solution)/shard_map/dot_general | solution.py:16
  16.6 57.3 %all_to_all.10 = bf16[16,64,2048]{2,1,0:T(8,128)(2,1)} all-to-all(bf16[16,64,2048]{2,1,0:T(8,128)(2,1)S(1)} %bitcast.52), channel_id=1, replica_groups=mesh['dp'=16,'expert'=16] {'expert'}, dimensions={0} | all-to-all | bytes 8388608 | tf_op jit(solution)/shard_map/all_to_all | solution.py:167
  73.9 1.6 all-gather.2.cloned.1.call-done.w_ref
  75.5 11.4 %hidden.1 = (bf16[512,768]{1,0:T(8,128)(2,1)S(1)}, bf16[512,768]{1,0:T(8,128)(2,1)S(1)}, bf16[512,768]{1,0:T(8,128)(2,1)S(1)}, f32[512,1]{1,0:T(8,128)}, bf16[51...) custom-call(s32[1]{0:T(128)} %bitcast.9.s_ref, ...), custom_call_target="tpu_custom_call" | custom-call | tf_op jit(solution)/shard_map/hidden/pallas_call | solution.py:75
  86.9 0.0 copy-start
  87.0 0.0 copy-start.1
  87.0 1.0 convolution_convert_fusion.6
  88.0 0.5 collective-permute-start
  88.4 1.0 convolution_convert_fusion.4
  89.5 0.2 collective-permute-start.1
  89.7 1.0 convolution_convert_fusion.2
  90.7 0.6 collective-permute-start.2
  91.4 0.1 collective-permute-done
  91.5 1.1 add_convert_fusion.2
  92.5 2.5 %dynamic_update_slice.9 = bf16[1024,2304]{1,0:T(8,128)(2,1)} pad(bf16[1024,768]{1,0:T(8,128)(2,1)S(1)} %add_convert_fusion.2, bf16[]{:T(256)} %constant.97.clone.1), padding=0_0x1536_0 | pad | bytes 6291458 | tf_op jit(solution)/shard_map/dynamic_update_slice | solution.py:200
  95.1 0.0 collective-permute-done.1
  95.1 0.0 copy-done
  95.1 2.3 %fusion.1 = bf16[1024,2304]{1,0:T(8,128)(2,1)} fusion(bf16[1024,2304]{1,0:T(8,128)(2,1)} %dynamic_update_slice.9, bf16[1024,768]{1,0:T(8,128)(2,1)S(1)} %collective-permute-done.1, bf16[512,1024]{1,0:T(8,128)(2,1)S(1)} %get-tuple-element.37, bf16[512,768]{1,0:T(8,128)(2,1)S(1)} %get-tuple-element.39.gate_ref), kind=kOutput, calls=%fused_computation.12 | convolution fusion | flops 809238528 | bytes 4980736 | tf_op jit(solution)/shard_map/dot_general | solution.py:20
  97.4 0.0 collective-permute-done.2
  97.4 0.0 copy-done.1
  97.4 2.2 %fusion.2 = bf16[1024,2304]{1,0:T(8,128)(2,1)} fusion(bf16[1024,2304]{1,0:T(8,128)(2,1)} %fusion.1, bf16[1024,768]{1,0:T(8,128)(2,1)S(1)} %collective-permute-done.2, bf16[512,1024]{1,0:T(8,128)(2,1)S(1)} %get-tuple-element.37, bf16[512,768]{1,0:T(8,128)(2,1)S(1)} %get-tuple-element.42.up_ref), kind=kOutput, calls=%fused_computation.13 | convolution fusion | flops 809238528 | bytes 4980736 | tf_op jit(solution)/shard_map/dot_general | solution.py:20
  99.6 0.0 reduce-scatter.2.cloned.1.call-update
  99.7 9.6 %route_back.1 = bf16[512,2304]{1,0:T(8,128)(2,1)} custom-call(bf16[512,768]{1,0:T(8,128)(2,1)} %copy-done, bf16[512,768]{1,0:T(8,128)(2,1)} %copy-done.1, bf16[3,2048,768]{2,1,0:T(8,128)(2,1)} %all-gather.2.cloned.1.call-done.w_ref, f32[512,1]{1,0:T(8,128)} %get-tuple-element.31.prob_ref), custom_call_target="tpu_custom_call" | custom-call | tf_op jit(solution)/shard_map/route_back/pallas_call | solution.py:111
  109.2 0.0 copy-start.2
  109.2 6.7 %all-to-all-start.1 = ((bf16[16,32,2304]{2,1,0:T(8,128)(2,1)}), bf16[16,32,2304]{2,1,0:T(8,128)(2,1)S(1)}, u32[]{:S(2)}, u32[]{:S(2)}) async-start(bf16[16,32,2304]{2,1,0:T(8,128)(2,1)} %bitcast.51), calls=%async_computation.1 | async-start | bytes 4718592 | tf_op jit(solution)/shard_map/all_to_all | solution.py:167
  115.9 36.3 %all-to-all-done.1 = bf16[16,32,2304]{2,1,0:T(8,128)(2,1)S(1)} async-done(((bf16[16,32,2304]{2,1,0:T(8,128)(2,1)}), bf16[16,32,2304]{2,1,0:T(8,128)(2,1)S(1)}, u32[]{:S(2)}, u32[]{:S(2)}) %all-to-all-start.1) | async-done | bytes 2359328 | tf_op jit(solution)/shard_map/all_to_all | solution.py:167
  152.3 0.1 convert_reduce_fusion
  152.4 0.2 select_reduce_fusion.1
  152.5 0.0 copy-done.2
  152.5 0.5 fusion.35
  153.1 1.3 convolution_convert_fusion.1
  154.3 4.6 %reduce-scatter.2.cloned.1.call-done = bf16[128,2304]{1,0:T(8,128)(2,1)} async-done(((bf16[1024,2304]{1,0:T(8,128)(2,1)}), bf16[128,2304]{1,0:T(8,128)(2,1)}) %reduce-scatter.2.cloned.1.call-update) | async-done | bytes 589840 | tf_op jit(solution)/shard_map/reduce_scatter | solution.py:201
  (9 shorter events, 0.1 us)
Async XLA Ops:
  7.2 68.4 %all-gather.2.cloned.1.call-start = ((), (), s32[]{:S(2)}) async-start(), calls=%async_computation.3 | async-start | bytes 10027008 | tf_op jit(solution)/shard_map/all_gather | solution.py:141
  9.2 149.7 %reduce-scatter.2.cloned.1.call-start = ((), (), s32[]{:S(2)}) async-start(), calls=%async_computation.4 | async-start | bytes 5308416 | tf_op jit(solution)/shard_map/reduce_scatter | solution.py:201
  86.9 8.1 %copy-start = (bf16[512,768]{1,0:T(8,128)(2,1)}, bf16[512,768]{1,0:T(8,128)(2,1)S(1)}, u32[]{:S(2)}) copy-start(bf16[512,768]{1,0:T(8,128)(2,1)S(1)} %get-tuple-element.39.gate_ref) | copy-start | bytes 2359300
  87.0 10.5 %copy-start.1 = (bf16[512,768]{1,0:T(8,128)(2,1)}, bf16[512,768]{1,0:T(8,128)(2,1)S(1)}, u32[]{:S(2)}) copy-start(bf16[512,768]{1,0:T(8,128)(2,1)S(1)} %get-tuple-element.42.up_ref) | copy-start | bytes 2359300
  88.0 3.5 %collective-permute-start = (bf16[1024,768]{1,0:T(8,128)(2,1)S(1)}, bf16[1024,768]{1,0:T(8,128)(2,1)S(1)}, u32[]{:S(2)}, u32[]{:S(2)}) collective-permute-start(bf16[1024,768]{1,0:T(8,128)(2,1)S(1)} %convolution_convert_fusion.6), channel_id=1, source_target_pairs={{0,16},{16,0},{32,48},{48,32},{64,80},{80,64},{96,112},{112,96},{1... | collective-permute-start | bytes 4718600 | tf_op jit(solution)/shard_map/ppermute | solution.py:183
  89.5 5.6 %collective-permute-start.1 = (bf16[1024,768]{1,0:T(8,128)(2,1)S(1)}, bf16[1024,768]{1,0:T(8,128)(2,1)S(1)}, u32[]{:S(2)}, u32[]{:S(2)}) collective-permute-start(bf16[1024,768]{1,0:T(8,128)(2,1)S(1)} %convolution_convert_fusion.4), channel_id=1, source_target_pairs={{0,16},{16,0},{32,48},{48,32},{64,80},{80,64},{96,112},{112,96},{1... | collective-permute-start | bytes 4718600 | tf_op jit(solution)/shard_map/ppermute | solution.py:183
  90.7 6.7 %collective-permute-start.2 = (bf16[1024,768]{1,0:T(8,128)(2,1)S(1)}, bf16[1024,768]{1,0:T(8,128)(2,1)S(1)}, u32[]{:S(2)}, u32[]{:S(2)}) collective-permute-start(bf16[1024,768]{1,0:T(8,128)(2,1)S(1)} %convolution_convert_fusion.2), channel_id=1, source_target_pairs={{0,16},{16,0},{32,48},{48,32},{64,80},{80,64},{96,112},{112,96},{1... | collective-permute-start | bytes 4718600 | tf_op jit(solution)/shard_map/ppermute | solution.py:183
  109.2 43.3 %copy-start.2 = (bf16[128,2]{0,1:T(2,128)(2,1)S(1)}, bf16[128,2]{0,1:T(2,128)(2,1)}, u32[]{:S(2)}) copy-start(bf16[128,2]{0,1:T(2,128)(2,1)} %param.11) | copy-start | bytes 1540
  109.2 43.0 %all-to-all-start.1 = ((bf16[16,32,2304]{2,1,0:T(8,128)(2,1)}), bf16[16,32,2304]{2,1,0:T(8,128)(2,1)S(1)}, u32[]{:S(2)}, u32[]{:S(2)}) async-start(bf16[16,32,2304]{2,1,0:T(8,128)(2,1)} %bitcast.51), calls=%async_computation.1 | async-start | bytes 4718592 | tf_op jit(solution)/shard_map/all_to_all | solution.py:167
Sparse Core Ops, SparseCore 0:
  10.4 65.0 all-gather.1
  99.8 59.0 reduce-scatter.1

commit v6 on v5

--- a/solution.py
+++ b/solution.py
@@ -43,7 +43,7 @@
         sig = jax.nn.sigmoid(gate)
         silu = gate * sig
         act = (silu * up).astype(BF16)
-        d_gate = (back * up * (sig * (1.0 + gate * (1.0 - sig)))).astype(BF16)
+        d_gate = (back * up * (sig + silu * (1.0 - sig))).astype(BF16)
         d_up = (back * silu).astype(BF16)
         for j in range(ff // BLOCK):
 
@@ -195,6 +195,7 @@
     own = [
         grad_of(lines, grad) for lines, grad in ((scaled_own, act), (rows_own, d_gate), (rows_own, d_up))
     ]
+    own = lax.optimization_barrier(own)
     pairs = jnp.zeros((chips * LANES, 3 * ff), BF16)
     for n, mine, theirs in zip((2, 0, 1), own, own_other, strict=True):
         pairs = lax.dynamic_update_slice(pairs, add(mine, theirs), (0, n * ff))

time: 166 us -> 167 us (level)
  other arithmetic: 4.89 us -> 8.65 us
  matrix products: 13 us -> 10.4 us
    dynamic_update_slice x0 -> x2, other arithmetic: none -> 3.35 us  [per_device(): pairs = lax.dynamic_update_slice(pairs, add(mine, theirs), (0, n * ff))]
    dot_general x7, matrix products: 9.95 us -> 7.39 us  [dot_rows(): lax.dot_general(left, right, (((0,), (0,)), ((), ())), preferred_element_...]
  transfers between devices with their start and end apart: 6 -> 6, of which waited for: 4 -> 3; matrix products, arithmetic and copies ran while one was open for 10% -> 11% of each run, Pallas kernels for 6% -> 6%
where the time goes in v6:
time: 167 us
  blocking collectives  57.3 us (34%)
  waiting for transfers between devices  42.4 us (25%)
  Pallas kernels  20.9 us (13%)
  between operations  14.8 us (9%)
  matrix products  10.4 us (6%)
  other arithmetic  8.65 us (5%)
  starting transfers between devices  7.95 us (5%)
  local copies, waits for them, and re-layouts  4.02 us (2%)
    all_to_all x1, blocking collectives, exchange(): lax.all_to_all(value.reshape(experts, lines, -1), 'expert', split_axis=0,...  57.3 us
    all_to_all x1, waiting for transfers between devices, exchange(): lax.all_to_all(value.reshape(experts, lines, -1), 'expert', split_axis=0,...  36.4 us
    pallas_call x1, Pallas kernels, hidden(): pl.pallas_call(body, grid_spec=pltpu.PrefetchScalarGridSpec(num_scalar_pr...  11.4 us
    pallas_call x1, Pallas kernels, route_back(): pl.pallas_call(body, grid=(steps + 1,), in_specs=[pl.BlockSpec((slots, ff...  9.56 us
    dot_general x7, matrix products, dot_rows(): lax.dot_general(left, right, (((0,), (0,)), ((), ())), preferred_element_...  7.39 us
    all_to_all x1, starting transfers between devices, exchange(): lax.all_to_all(value.reshape(experts, lines, -1), 'expert', split_axis=0,...  6.55 us
    reduce_scatter x1, waiting for transfers between devices, per_device(): lax.psum_scatter(pairs, 'dp', scatter_dimension=0, axis_index_groups=[[2...  4.45 us
    dynamic_update_slice x2, other arithmetic, per_device(): pairs = lax.dynamic_update_slice(pairs, add(mine, theirs), (0, n * ff))  3.35 us
  transfers between devices with their start and end apart: 6, of which 3 were waited for; matrix products, arithmetic and copies ran while one was open for 11% of the time, Pallas kernels for 6%

profile of v6, /device:TPU:1, one launch (start us, length us, event | category | flops | bytes accessed | tf_op | source)
XLA Modules:
  0.0 166.6 jit_solution(12949435841582049043)
XLA Ops:
  7.2 0.0 all-gather.2.cloned.1.call-start
  7.2 2.0 %pad_maximum_fusion = bf16[3,128,768]{2,1,0:T(8,128)(2,1)} fusion(bf16[1,128,768]{2,1,0:T(8,128)(2,1)} %param.15, bf16[1,128,768]{2,1,0:T(8,128)(2,1)} %param.14, bf16[1,128,768]{2,1,0:T(8,128)(2,1)} %param.13), kind=kLoop, calls=%fused_computation.20 | loop fusion | flops 589824 | bytes 1179648 | tf_op jit(solution)/shard_map/concatenate | solution.py:142
  9.2 0.0 all-gather.2.cloned.1.call-update
  9.2 0.0 reduce-scatter.2.cloned.1.call-start
  9.3 0.8 copy.36
  10.1 0.1 eq.122
  10.2 0.1 eq.118
  11.0 0.6 reduce-window.6
  11.6 0.2 slice_reduce_fusion
  11.8 0.1 fusion.20
  11.9 0.1 reduce_sum.30
  12.1 0.1 copy.39
  12.2 0.7 convert_select_fusion
  12.9 0.7 multiply_add_fusion
  13.5 3.0 %convolution_convert_fusion = bf16[1024,2048]{1,0:T(8,128)(2,1)S(1)} fusion(bf16[128,2048]{1,0:T(8,128)(2,1)} %param.9, bf16[128,2048]{1,0:T(8,128)(2,1)} %param.8, f32[256]{0:T(256)S(1)} %bitcast.58, s32[256]{0:T(256)S(1)} %bitcast.60, f32[256]{0:T(256)S(1)} %bitcast.57, s32[256]{0:T(256)S(1)} %and_select_fusion, s32[256]{0:T(256)S(1)} %bitcast.59, ...), kind=kOutput, calls=%fused_computation | convolution fusion | flops 1080295424 | bytes 5256192 | tf_op jit(solution)/shard_map/dot_general | solution.py:16
  16.6 57.3 %all_to_all.10 = bf16[16,64,2048]{2,1,0:T(8,128)(2,1)} all-to-all(bf16[16,64,2048]{2,1,0:T(8,128)(2,1)S(1)} %bitcast.52), channel_id=1, replica_groups=mesh['dp'=16,'expert'=16] {'expert'}, dimensions={0} | all-to-all | bytes 8388608 | tf_op jit(solution)/shard_map/all_to_all | solution.py:167
  73.9 1.6 all-gather.2.cloned.1.call-done.w_ref
  75.5 11.4 %hidden.1 = (bf16[512,768]{1,0:T(8,128)(2,1)S(1)}, bf16[512,768]{1,0:T(8,128)(2,1)S(1)}, bf16[512,768]{1,0:T(8,128)(2,1)S(1)}, f32[512,1]{1,0:T(8,128)}, bf16[51...) custom-call(s32[1]{0:T(128)} %bitcast.9.s_ref, ...), custom_call_target="tpu_custom_call" | custom-call | tf_op jit(solution)/shard_map/hidden/pallas_call | solution.py:75
  86.9 0.0 copy-start.1
  86.9 0.0 copy-start
  86.9 1.0 convolution_convert_fusion.4
  87.9 0.5 collective-permute-start
  88.4 1.0 convolution_convert_fusion.3
  89.4 0.2 collective-permute-start.1
  89.6 1.0 convolution_convert_fusion.2
  90.7 0.6 collective-permute-start.2
  91.3 0.0 copy-done.1
  91.3 1.0 convolution_convert_fusion.5
  92.3 0.0 copy-done
  92.3 1.0 convolution_convert_fusion.6
  93.4 1.0 convolution_convert_fusion.7
  94.4 0.0 collective-permute-done
  94.4 0.4 add_convert_fusion.2
  94.8 2.5 %dynamic_update_slice.9 = bf16[1024,2304]{1,0:T(8,128)(2,1)} pad(bf16[1024,768]{1,0:T(8,128)(2,1)S(1)} %add_convert_fusion.2, bf16[]{:T(256)} %constant.97.clone.1), padding=0_0x1536_0 | pad | bytes 6291458 | tf_op jit(solution)/shard_map/dynamic_update_slice | solution.py:201
  97.4 0.0 collective-permute-done.1
  97.4 1.7 %fusion.1 = bf16[1024,2304]{1,0:T(8,128)(2,1)} fusion(bf16[1024,2304]{1,0:T(8,128)(2,1)} %dynamic_update_slice.9, bf16[1024,768]{1,0:T(8,128)(2,1)S(1)} %collective-permute-done.1, bf16[1024,768]{1,0:T(8,128)(2,1)S(1)} %convolution_convert_fusion.6), kind=kLoop, calls=%fused_computation.12 | loop fusion | flops 3145728 | bytes 4718592 | tf_op jit(solution)/shard_map/dynamic_update_slice | solution.py:201
  99.1 0.0 collective-permute-done.2
  99.1 1.6 fusion.2
  100.7 0.0 reduce-scatter.2.cloned.1.call-update
  100.7 9.6 %route_back.1 = bf16[512,2304]{1,0:T(8,128)(2,1)} custom-call(bf16[512,768]{1,0:T(8,128)(2,1)} %copy-done, bf16[512,768]{1,0:T(8,128)(2,1)} %copy-done.1, bf16[3,2048,768]{2,1,0:T(8,128)(2,1)} %all-gather.2.cloned.1.call-done.w_ref, f32[512,1]{1,0:T(8,128)} %get-tuple-element.34.prob_ref), custom_call_target="tpu_custom_call" | custom-call | tf_op jit(solution)/shard_map/route_back/pallas_call | solution.py:111
  110.3 6.5 %all-to-all-start.1 = ((bf16[16,32,2304]{2,1,0:T(8,128)(2,1)}), bf16[16,32,2304]{2,1,0:T(8,128)(2,1)S(1)}, u32[]{:S(2)}, u32[]{:S(2)}) async-start(bf16[16,32,2304]{2,1,0:T(8,128)(2,1)} %bitcast.51), calls=%async_computation.1 | async-start | bytes 4718592 | tf_op jit(solution)/shard_map/all_to_all | solution.py:167
  116.9 36.4 %all-to-all-done.1 = bf16[16,32,2304]{2,1,0:T(8,128)(2,1)S(1)} async-done(((bf16[16,32,2304]{2,1,0:T(8,128)(2,1)}), bf16[16,32,2304]{2,1,0:T(8,128)(2,1)S(1)}, u32[]{:S(2)}, u32[]{:S(2)}) %all-to-all-start.1) | async-done | bytes 2359328 | tf_op jit(solution)/shard_map/all_to_all | solution.py:167
  153.2 0.1 convert_reduce_fusion
  153.3 0.2 select_reduce_fusion.1
  153.5 0.0 copy-done.2
  153.5 0.5 fusion.35
  154.0 1.3 convolution_convert_fusion.1
  155.3 4.4 %reduce-scatter.2.cloned.1.call-done = bf16[128,2304]{1,0:T(8,128)(2,1)} async-done(((bf16[1024,2304]{1,0:T(8,128)(2,1)}), bf16[128,2304]{1,0:T(8,128)(2,1)}) %reduce-scatter.2.cloned.1.call-update) | async-done | bytes 589840 | tf_op jit(solution)/shard_map/reduce_scatter | solution.py:202
  (10 shorter events, 0.1 us)
Async XLA Ops:
  7.2 68.4 %all-gather.2.cloned.1.call-start = ((), (), s32[]{:S(2)}) async-start(), calls=%async_computation.3 | async-start | bytes 10027008 | tf_op jit(solution)/shard_map/all_gather | solution.py:141
  9.2 150.5 %reduce-scatter.2.cloned.1.call-start = ((), (), s32[]{:S(2)}) async-start(), calls=%async_computation.4 | async-start | bytes 5308416 | tf_op jit(solution)/shard_map/reduce_scatter | solution.py:202
  86.9 4.4 %copy-start.1 = (bf16[512,768]{1,0:T(8,128)(2,1)}, bf16[512,768]{1,0:T(8,128)(2,1)S(1)}, u32[]{:S(2)}) copy-start(bf16[512,768]{1,0:T(8,128)(2,1)S(1)} %get-tuple-element.48.up_ref) | copy-start | bytes 2359300
  86.9 5.4 %copy-start = (bf16[512,768]{1,0:T(8,128)(2,1)}, bf16[512,768]{1,0:T(8,128)(2,1)S(1)}, u32[]{:S(2)}) copy-start(bf16[512,768]{1,0:T(8,128)(2,1)S(1)} %get-tuple-element.44.gate_ref) | copy-start | bytes 2359300
  87.9 6.5 %collective-permute-start = (bf16[1024,768]{1,0:T(8,128)(2,1)S(1)}, bf16[1024,768]{1,0:T(8,128)(2,1)S(1)}, u32[]{:S(2)}, u32[]{:S(2)}) collective-permute-start(bf16[1024,768]{1,0:T(8,128)(2,1)S(1)} %convolution_convert_fusion.4), channel_id=1, source_target_pairs={{0,16},{16,0},{32,48},{48,32},{64,80},{80,64},{96,112},{112,96},{1... | collective-permute-start | bytes 4718600 | tf_op jit(solution)/shard_map/ppermute | solution.py:183
  89.4 8.0 %collective-permute-start.1 = (bf16[1024,768]{1,0:T(8,128)(2,1)S(1)}, bf16[1024,768]{1,0:T(8,128)(2,1)S(1)}, u32[]{:S(2)}, u32[]{:S(2)}) collective-permute-start(bf16[1024,768]{1,0:T(8,128)(2,1)S(1)} %convolution_convert_fusion.3), channel_id=1, source_target_pairs={{0,16},{16,0},{32,48},{48,32},{64,80},{80,64},{96,112},{112,96},{1... | collective-permute-start | bytes 4718600 | tf_op jit(solution)/shard_map/ppermute | solution.py:183
  90.7 8.4 %collective-permute-start.2 = (bf16[1024,768]{1,0:T(8,128)(2,1)S(1)}, bf16[1024,768]{1,0:T(8,128)(2,1)S(1)}, u32[]{:S(2)}, u32[]{:S(2)}) collective-permute-start(bf16[1024,768]{1,0:T(8,128)(2,1)S(1)} %convolution_convert_fusion.2), channel_id=1, source_target_pairs={{0,16},{16,0},{32,48},{48,32},{64,80},{80,64},{96,112},{112,96},{1... | collective-permute-start | bytes 4718600 | tf_op jit(solution)/shard_map/ppermute | solution.py:183
  110.3 43.2 %copy-start.2 = (bf16[128,2]{0,1:T(2,128)(2,1)S(1)}, bf16[128,2]{0,1:T(2,128)(2,1)}, u32[]{:S(2)}) copy-start(bf16[128,2]{0,1:T(2,128)(2,1)} %param.11) | copy-start | bytes 1540
  110.3 42.9 %all-to-all-start.1 = ((bf16[16,32,2304]{2,1,0:T(8,128)(2,1)}), bf16[16,32,2304]{2,1,0:T(8,128)(2,1)S(1)}, u32[]{:S(2)}, u32[]{:S(2)}) async-start(bf16[16,32,2304]{2,1,0:T(8,128)(2,1)} %bitcast.51), calls=%async_computation.1 | async-start | bytes 4718592 | tf_op jit(solution)/shard_map/all_to_all | solution.py:167
Sparse Core Ops, SparseCore 0:
  10.4 65.0 all-gather.1
  100.9 58.8 reduce-scatter.1
